TPU v7x, 256 devices: a whole 4x4x8 slice. The times are simulated.
256 devices in a mesh: dp: 4 (over x_hi, core), row: 8 (over z), col: 8 (over x_lo, y).
Axes of the slice: x: 4 (x_hi: 2, x_lo: 2; x = x_hi * 2 + x_lo), y: 4, z: 8, core: 2. Of those that a mesh axis runs over, the one named last changes fastest.
Arguments:
- tokens: bfloat16 [4096, 4096], P(('dp', 'col'), 'row'), may hold values from -6 to 6
- cotangent: bfloat16 [4096, 4096], P(('dp', 'col'), 'row'), may hold values from -6 to 6
- gate_pre: bfloat16 [4096, 14336], P(('dp', 'row'), 'col'), may hold values from -6 to 6
- up_pre: bfloat16 [4096, 14336], P(('dp', 'row'), 'col'), may hold values from -6 to 6
- w_gate: bfloat16 [14336, 4096], P('col', 'row'), may hold values from -0.09375 to 0.09375
- w_up: bfloat16 [14336, 4096], P('col', 'row'), may hold values from -0.09375 to 0.09375
- w_down: bfloat16 [4096, 14336], P('row', 'col'), may hold values from -0.046875 to 0.046875
Outputs:
- d_tokens: bfloat16 [4096, 4096], P(('dp', 'col'), 'row')
- grad_gate: float32 [14336, 4096], P(('col', 'dp'), 'row')
- grad_up: float32 [14336, 4096], P(('col', 'dp'), 'row')
- grad_down: float32 [4096, 14336], P(('row', 'dp'), 'col')
All inputs are finite; a program needn't handle non-finite values.
Results may differ from a plain program's by a relative error of at most 0.02.
Values may be sent and summed in bfloat16 or wider, within the bound.
No kernel may reach another device: no remote copies, remote signals or barrier semaphores. Data moves between devices by JAX's collectives and lax.ppermute only.
A program may use at most 128 MiB of HBM per device.

v0:
```python
import jax
import jax.numpy as jnp
from jax import lax
from jax.sharding import PartitionSpec as P


def contract_tokens(left, right):
    return lax.dot_general(
        left, right, (((0,), (0,)), ((), ())), preferred_element_type=jnp.float32
    )


def local_grads(hidden_grad, gate_pre, up_pre):
    gate_value = gate_pre.astype(jnp.float32)
    up_value = up_pre.astype(jnp.float32)
    sigmoid_gate = jax.nn.sigmoid(gate_value)
    hidden = (gate_value * sigmoid_gate * up_value).astype(jnp.bfloat16)
    gate_grad = (
        hidden_grad * up_value * sigmoid_gate * (1.0 + gate_value * (1.0 - sigmoid_gate))
    ).astype(jnp.bfloat16)
    up_grad = (hidden_grad * gate_value * sigmoid_gate).astype(jnp.bfloat16)
    return (hidden, gate_grad, up_grad)


def local(tokens, cotangent, gate_pre, up_pre, w_gate, w_up, w_down):
    tok_cols, cot_cols = (
        lax.all_gather(tokens, "col", axis=0, tiled=True),
        lax.all_gather(cotangent, "col", axis=0, tiled=True),
    )
    partial_grad = jnp.dot(cot_cols, w_down, preferred_element_type=jnp.float32)
    hidden_grad = lax.psum(partial_grad.astype(jnp.bfloat16), "row").astype(jnp.float32)
    gate_all, up_all = (
        lax.all_gather(gate_pre, "row", axis=0, tiled=True),
        lax.all_gather(up_pre, "row", axis=0, tiled=True),
    )
    hidden, gate_grad, up_grad = local_grads(hidden_grad, gate_all, up_all)
    d_tokens = lax.psum_scatter(
        (
            jnp.dot(gate_grad, w_gate, preferred_element_type=jnp.float32)
            + jnp.dot(up_grad, w_up, preferred_element_type=jnp.float32)
        ).astype(jnp.bfloat16),
        "col",
        scatter_dimension=0,
        tiled=True,
    )
    grad_down = lax.psum_scatter(
        contract_tokens(cot_cols, hidden).astype(jnp.bfloat16),
        "dp",
        scatter_dimension=0,
        tiled=True,
    ).astype(jnp.float32)
    feature_count = w_gate.shape[1]
    stacked = lax.psum_scatter(
        jnp.concatenate(
            [contract_tokens(gate_grad, tok_cols), contract_tokens(up_grad, tok_cols)], axis=1
        ).astype(jnp.bfloat16),
        "dp",
        scatter_dimension=0,
        tiled=True,
    ).astype(jnp.float32)
    grad_gate = stacked[:, :feature_count]
    grad_up = stacked[:, feature_count:]
    return (d_tokens, grad_gate, grad_up, grad_down)


def solution(mesh):
    placed = (
        P(("dp", "col"), "row"),
        P(("dp", "col"), "row"),
        P(("dp", "row"), "col"),
        P(("dp", "row"), "col"),
        P("col", "row"),
        P("col", "row"),
        P("row", "col"),
    )
    return jax.shard_map(
        local,
        mesh=mesh,
        in_specs=placed,
        out_specs=(
            P(("dp", "col"), "row"),
            P(("col", "dp"), "row"),
            P(("col", "dp"), "row"),
            P(("row", "dp"), "col"),
        ),
        check_vma=False,
    )
```

profile of v0, /device:TPU:8, one launch (start us, length us, event | category | flops | bytes accessed | tf_op | source)
XLA Modules:
  0.0 445.3 jit_solution(11085456444376868423)
XLA Ops:
  7.2 0.0 copy-start
  7.2 0.0 all-gather.5.cloned.1.call-start
  7.2 0.7 all-gather.5.cloned.1.call-update
  7.9 0.0 all-gather.9.cloned.1.call-start
  8.0 0.7 all-gather.9.cloned.1.call-update
  8.7 0.0 all-gather.7.cloned.1.call-start
  8.7 0.7 all-gather.7.cloned.1.call-update
  9.4 0.0 all-reduce.2.cloned.1.call-start
  9.4 42.4 %all-gather.5.cloned.1.call-done = bf16[1024,512]{1,0:T(8,128)(2,1)} async-done(((bf16[128,512]{1,0:T(8,128)(2,1)}), bf16[1024,512]{1,0:T(8,128)(2,1)}) %all-gather.5.cloned.1.call-update) | async-done | bytes 1048592 | tf_op jit(solution)/shard_map/all_gather | solution.py:28
  51.8 0.0 copy-done
  51.8 5.2 %convolution_convert_fusion = bf16[1024,1792]{1,0:T(8,128)(2,1)} fusion(bf16[1024,512]{1,0:T(8,128)(2,1)} %all-gather.5.cloned.1.call-done, bf16[512,1792]{1,0:T(8,128)(2,1)S(1)} %copy-done), kind=kOutput, calls=%fused_computation.16 | convolution fusion | flops 1880883200 | bytes 6553600 | tf_op jit(solution)/shard_map/dot_general | solution.py:30
  57.1 0.0 copy-start.4
  57.1 0.0 all-reduce.2.cloned.1.call-update
  57.1 0.0 all-gather.11.cloned.1.call-start
  57.1 0.5 all-gather.11.cloned.1.call-update
  57.7 0.0 reduce-scatter.12.cloned.1.call-start
  57.7 47.3 %all-gather.9.cloned.1.call-done = bf16[1024,1792]{1,0:T(8,128)(2,1)} async-done(((bf16[128,1792]{1,0:T(8,128)(2,1)}), bf16[1024,1792]{1,0:T(8,128)(2,1)}) %all-gather.9.cloned.1.call-update) | async-done | bytes 3670032 | tf_op jit(solution)/shard_map/all_gather | solution.py:33
  105.0 50.3 %all-gather.7.cloned.1.call-done = bf16[1024,1792]{1,0:T(8,128)(2,1)} async-done(((bf16[128,1792]{1,0:T(8,128)(2,1)}), bf16[1024,1792]{1,0:T(8,128)(2,1)}) %all-gather.7.cloned.1.call-update) | async-done | bytes 3670032 | tf_op jit(solution)/shard_map/all_gather | solution.py:34
  155.3 0.0 copy-done.4
  155.3 7.3 %fusion.15 = bf16[512,1792]{0,1:T(8,128)(2,1)} fusion(bf16[1024,512]{1,0:T(8,128)(2,1)S(1)} %copy-done.4, bf16[1024,1792]{1,0:T(8,128)(2,1)} %all-gather.7.cloned.1.call-done, bf16[1024,1792]{1,0:T(8,128)(2,1)} %all-gather.9.cloned.1.call-done), kind=kOutput, calls=%fused_computation.22 | convolution fusion | flops 1894645760 | bytes 10223616 | tf_op jit(solution)/shard_map/dot_general | solution.py:8
  162.7 3.8 copy.19
  166.5 0.0 reduce-scatter.12.cloned.1.call-update
  166.5 0.2 reduce-scatter.10.cloned.1.call-start
  166.7 88.9 %all-reduce.2.cloned.1.call-done = bf16[1024,1792]{1,0:T(8,128)(2,1)} async-done(((bf16[1024,1792]{1,0:T(8,128)(2,1)}), bf16[1024,1792]{1,0:T(8,128)(2,1)}) %all-reduce.2.cloned.1.call-update) | async-done | bytes 3670032 | tf_op jit(solution)/shard_map/psum | solution.py:31
  255.7 8.3 %fusion.9 = (bf16[1024,1792]{1,0:T(8,128)(2,1)}, bf16[1024,1792]{1,0:T(8,128)(2,1)}) fusion(bf16[1024,1792]{1,0:T(8,128)(2,1)} %all-gather.9.cloned.1.call-done, bf16[1024,1792]{1,0:T(8,128)(2,1)} %all-reduce.2.cloned.1.call-done, bf16[1024,1792]{1,0:T(8,128)(2,1)} %all-gather.7.cloned.1.call-done), kind=kLoop, calls=%fused_computation.15 | loop fusion | flops 29360128 | bytes 18350080 | tf_op jit(solution)/shard_map/convert_element_type | solution.py:21
  264.0 31.2 %all-gather.11.cloned.1.call-done = bf16[1024,512]{1,0:T(8,128)(2,1)} async-done(((bf16[128,512]{1,0:T(8,128)(2,1)}), bf16[1024,512]{1,0:T(8,128)(2,1)}) %all-gather.11.cloned.1.call-update) | async-done | bytes 1048592 | tf_op jit(solution)/shard_map/all_gather | solution.py:27
  295.1 0.0 copy-start.2
  295.1 0.0 copy-start.5
  295.1 4.6 %convolution_convert_fusion.1 = bf16[1792,512]{0,1:T(8,128)(2,1)S(1)} fusion(bf16[1024,1792]{1,0:T(8,128)(2,1)} %get-tuple-element.12, bf16[1024,512]{1,0:T(8,128)(2,1)} %all-gather.11.cloned.1.call-done), kind=kOutput, calls=%fused_computation.20 | convolution fusion | flops 1879965696 | bytes 6553600 | tf_op jit(solution)/shard_map/dot_general | solution.py:8
  299.7 0.0 copy-done.2
  299.7 0.0 copy-done.5
  299.8 2.2 convolution_convert_fusion.2
  302.0 2.1 pad_maximum_fusion
  304.0 5.9 %copy.17 = bf16[1792,1024]{1,0:T(8,128)(2,1)} copy(bf16[1792,1024]{0,1:T(8,128)(2,1)} %pad_maximum_fusion) | data formatting | bytes 7340032
  310.0 0.0 reduce-scatter.10.cloned.1.call-update
  310.0 0.0 reduce-scatter.8.cloned.1.call-start
  310.1 0.0 copy-start.1
  310.1 0.0 copy-start.3
  310.1 5.3 %fusion.20 = f32[1024,512]{1,0:T(8,128)S(1)} fusion(bf16[1024,1792]{1,0:T(8,128)(2,1)} %get-tuple-element.13, bf16[1792,512]{1,0:T(8,128)(2,1)} %param.11), kind=kOutput, calls=%fused_computation.26 | convolution fusion | flops 1879048192 | bytes 7602176 | tf_op jit(solution)/shard_map/dot_general | solution.py:39
  315.3 0.0 copy-done.1
  315.3 0.0 copy-done.3
  315.4 3.0 add_convert_fusion
  318.4 0.0 reduce-scatter.8.cloned.1.call-update
  318.4 22.7 %reduce-scatter.12.cloned.1.call-done = bf16[128,1792]{1,0:T(8,128)(2,1)} async-done(((bf16[512,1792]{1,0:T(8,128)(2,1)}), bf16[128,1792]{1,0:T(8,128)(2,1)}) %reduce-scatter.12.cloned.1.call-update) | async-done | bytes 458768
  341.1 1.3 copy.20
  342.4 1.1 copy.16
  343.5 53.4 %reduce-scatter.10.cloned.1.call-done = bf16[448,1024]{1,0:T(8,128)(2,1)} async-done(((bf16[1792,1024]{1,0:T(8,128)(2,1)}), bf16[448,1024]{1,0:T(8,128)(2,1)}) %reduce-scatter.10.cloned.1.call-update) | async-done | bytes 917520
  396.9 1.5 copy.18
  398.4 1.6 fusion.19
  400.0 2.5 copy.14
  402.5 2.5 copy.15
  404.9 33.5 %reduce-scatter.8.cloned.1.call-done = bf16[128,512]{1,0:T(8,128)(2,1)} async-done(((bf16[1024,512]{1,0:T(8,128)(2,1)}), bf16[128,512]{1,0:T(8,128)(2,1)}) %reduce-scatter.8.cloned.1.call-update) | async-done | bytes 131088 | tf_op jit(solution)/shard_map/reduce_scatter | solution.py:37
Async XLA Ops:
  7.2 44.7 %copy-start = (bf16[512,1792]{1,0:T(8,128)(2,1)S(1)}, bf16[512,1792]{1,0:T(8,128)(2,1)}, u32[]{:S(2)}) copy-start(bf16[512,1792]{1,0:T(8,128)(2,1)} %param.13) | copy-start | bytes 5505028
  7.2 44.7 %all-gather.5.cloned.1.call-start = ((), (), s32[]{:S(2)}) async-start(), calls=%async_computation.3 | async-start | bytes 1179648 | tf_op jit(solution)/shard_map/all_gather | solution.py:28
  7.9 97.1 %all-gather.9.cloned.1.call-start = ((), (), s32[]{:S(2)}) async-start(), calls=%async_computation.6 | async-start | bytes 4128768 | tf_op jit(solution)/shard_map/all_gather | solution.py:33
  8.7 146.7 %all-gather.7.cloned.1.call-start = ((), (), s32[]{:S(2)}) async-start(), calls=%async_computation.5 | async-start | bytes 4128768 | tf_op jit(solution)/shard_map/all_gather | solution.py:34
  9.4 246.3 %all-reduce.2.cloned.1.call-start = ((), (), s32[]{:S(2)}) async-start(), calls=%async_computation.4 | async-start | bytes 7340032 | tf_op jit(solution)/shard_map/psum | solution.py:31
  57.1 98.3 %copy-start.4 = (bf16[1024,512]{1,0:T(8,128)(2,1)S(1)}, bf16[1024,512]{1,0:T(8,128)(2,1)}, u32[]{:S(2)}) copy-start(bf16[1024,512]{1,0:T(8,128)(2,1)} %all-gather.5.cloned.1.call-done) | copy-start | bytes 3145732
  57.1 238.1 %all-gather.11.cloned.1.call-start = ((), (), s32[]{:S(2)}) async-start(), calls=%async_computation.8 | async-start | bytes 1179648 | tf_op jit(solution)/shard_map/all_gather | solution.py:27
  57.7 283.4 %reduce-scatter.12.cloned.1.call-start = ((), (), s32[]{:S(2)}) async-start(), calls=%async_computation.10 | async-start | bytes 2293760
  166.5 230.4 %reduce-scatter.10.cloned.1.call-start = ((), (), s32[]{:S(2)}) async-start(), calls=%async_computation.9 | async-start | bytes 4587520
  295.1 4.6 %copy-start.2 = (bf16[1024,1792]{1,0:T(8,128)(2,1)S(1)}, bf16[1024,1792]{1,0:T(8,128)(2,1)}, u32[]{:S(2)}) copy-start(bf16[1024,1792]{1,0:T(8,128)(2,1)} %get-tuple-element.13) | copy-start | bytes 11010052
  295.1 4.6 %copy-start.5 = (bf16[1024,512]{1,0:T(8,128)(2,1)S(1)}, bf16[1024,512]{1,0:T(8,128)(2,1)}, u32[]{:S(2)}) copy-start(bf16[1024,512]{1,0:T(8,128)(2,1)} %all-gather.11.cloned.1.call-done) | copy-start | bytes 3145732
  310.0 128.5 %reduce-scatter.8.cloned.1.call-start = ((), (), s32[]{:S(2)}) async-start(), calls=%async_computation.7 | async-start | bytes 1179648 | tf_op jit(solution)/shard_map/reduce_scatter | solution.py:37
  310.1 5.3 %copy-start.1 = (bf16[1024,1792]{1,0:T(8,128)(2,1)S(1)}, bf16[1024,1792]{1,0:T(8,128)(2,1)}, u32[]{:S(2)}) copy-start(bf16[1024,1792]{1,0:T(8,128)(2,1)} %get-tuple-element.12) | copy-start | bytes 11010052
  310.1 5.3 %copy-start.3 = (bf16[1792,512]{1,0:T(8,128)(2,1)S(1)}, bf16[1792,512]{1,0:T(8,128)(2,1)}, u32[]{:S(2)}) copy-start(bf16[1792,512]{1,0:T(8,128)(2,1)} %param.12) | copy-start | bytes 5505028
Sparse Core Ops, SparseCore 0:
  9.8 41.9 all-gather.4
  53.6 51.3 all-gather.8
  106.8 48.4 all-gather.6
  157.6 98.0 all-reduce.1
  257.3 37.7 all-gather.10
  297.8 43.2 reduce-scatter.11
  344.1 52.7 reduce-scatter.9
  400.0 38.4 reduce-scatter.7
where the time goes:
time: 448 us; the launch traced here: 445 us
  waiting for transfers between devices  372 us (83%)
  matrix products  27.6 us (6%)
  local copies, waits for them, and re-layouts  20.2 us (5%)
  between operations  14.2 us (3%)
  other arithmetic  10.4 us (2%)
    psum x1, waiting for transfers between devices, local(): lax.psum(partial_grad.astype(jnp.bfloat16), 'row').astype(jnp.float32)  88.9 us
    unnamed x10, waiting for transfers between devices  78.7 us
    all_gather x1, waiting for transfers between devices, local(): lax.all_gather(up_pre, 'row', axis=0, tiled=True)  50.3 us
    all_gather x1, waiting for transfers between devices, local(): lax.all_gather(gate_pre, 'row', axis=0, tiled=True)  47.3 us
    all_gather x1, waiting for transfers between devices, local(): lax.all_gather(cotangent, 'col', axis=0, tiled=True)  42.4 us
    reduce_scatter x1, waiting for transfers between devices, local(): lax.psum_scatter((jnp.dot(gate_grad, w_gate, preferred_element_type=jnp.f...  33.5 us
    all_gather x1, waiting for transfers between devices, local(): lax.all_gather(tokens, 'col', axis=0, tiled=True)  31.2 us
    unnamed x19, local copies, waits for them, and re-layouts  18.6 us
  transfers between devices with their start and end apart: 8, of which 8 were waited for; matrix products, arithmetic and copies ran while one was open for 13% of the time, Pallas kernels for 0%

commit v1 on v0

v1 whole, which is shorter than its diff:
```python
import jax
import jax.numpy as jnp
from jax import lax
from jax.sharding import PartitionSpec as P

F32 = jnp.float32
BF16 = jnp.bfloat16
ROWS = 8


def shift_row(x, step):
    return lax.ppermute(x, "row", [(i, (i + step) % ROWS) for i in range(ROWS)])


def exchange(x, axis, groups=None):
    return lax.all_to_all(x, axis, 0, 0, axis_index_groups=groups, tiled=True)


def gather_col(x):
    return exchange(jnp.broadcast_to(x, (8,) + x.shape), "col").reshape(-1, x.shape[-1])


def sum_dp(x):
    near = exchange(jnp.swapaxes(x.astype(BF16), 0, 1), "dp", [[0, 1], [2, 3]])
    half = (near[0].astype(F32) + near[1].astype(F32)).astype(BF16)
    far = exchange(half, "dp", [[0, 2], [1, 3]])
    return far[0].astype(F32) + far[1].astype(F32)


def gather_row(x, sign):
    blocks = [None] * ROWS
    blocks[0] = up = down = x
    for step in range(1, 5):
        if step < 4 or sign > 0:
            up = shift_row(up, 1)
            blocks[ROWS - step] = up
        if step < 4 or sign < 0:
            down = shift_row(down, -1)
            blocks[step] = down
    return blocks


def contract_tokens(left, right):
    return lax.dot_general(left, right, (((0,), (0,)), ((), ())), preferred_element_type=F32)


def local(tokens, cotangent, gate_pre, up_pre, w_gate, w_up, w_down):
    row = lax.axis_index("row")
    block, hidden_width = gate_pre.shape
    features = w_gate.shape[1]

    def turned(x, by):
        twice = jnp.concatenate([x, x], axis=0)
        return lax.dynamic_slice_in_dim(twice, by * block, ROWS * block, 0)

    gate_value = gate_pre.astype(F32)
    up_value = up_pre.astype(F32)
    sigmoid_gate = jax.nn.sigmoid(gate_value)
    hidden = (gate_value * sigmoid_gate * up_value).astype(BF16)
    hidden_blocks = gather_row(hidden, 1)

    cot = gather_col(cotangent)
    cot, hidden_blocks[1], hidden_blocks[7] = lax.optimization_barrier(
        (cot, hidden_blocks[1], hidden_blocks[7])
    )
    partial = jnp.dot(cot, w_down, preferred_element_type=F32).astype(BF16)
    partial, tokens = lax.optimization_barrier((partial, tokens))
    hidden_grad = lax.psum_scatter(partial, "row", scatter_dimension=0, tiled=True)
    hidden_grad, *hidden_blocks = lax.optimization_barrier((hidden_grad, *hidden_blocks))
    hidden_grad = hidden_grad.astype(F32)
    gate_grad = (
        hidden_grad * up_value * sigmoid_gate * (1.0 + gate_value * (1.0 - sigmoid_gate))
    ).astype(BF16)
    up_grad = (hidden_grad * gate_value * sigmoid_gate).astype(BF16)
    gate_all = lax.all_gather(gate_grad, "row", axis=0, tiled=True)
    up_all = jnp.concatenate(gather_row(up_grad, -1), axis=0)

    hidden_all = jnp.concatenate(hidden_blocks, axis=0)
    grad_down = sum_dp(
        contract_tokens(turned(cot, row), hidden_all).reshape(2, 2, block, hidden_width)
    )
    tok = gather_col(tokens)
    grad_up = sum_dp(contract_tokens(up_all, turned(tok, row)).reshape(2, 2, -1, features))
    grad_gate = sum_dp(contract_tokens(gate_all, tok).reshape(2, 2, -1, features))
    from_up = jnp.dot(up_all, w_up, preferred_element_type=F32)
    from_gate = jnp.dot(gate_all, w_gate, preferred_element_type=F32)
    token_grad = (from_gate + turned(from_up, (ROWS - row) & 7)).astype(BF16)
    token_grad = exchange(token_grad.reshape(8, block, features), "col")
    d_tokens = jnp.sum(token_grad.astype(F32), axis=0).astype(BF16)
    return (d_tokens, grad_gate, grad_up, grad_down)


def solution(mesh):
    placed = (
        P(("dp", "col"), "row"),
        P(("dp", "col"), "row"),
        P(("dp", "row"), "col"),
        P(("dp", "row"), "col"),
        P("col", "row"),
        P("col", "row"),
        P("row", "col"),
    )
    return jax.shard_map(
        local,
        mesh=mesh,
        in_specs=placed,
        out_specs=(
            P(("dp", "col"), "row"),
            P(("col", "dp"), "row"),
            P(("col", "dp"), "row"),
            P(("row", "dp"), "col"),
        ),
        check_vma=False,
    )
```

time: 448 us -> 296 us (0.66)
  waiting for transfers between devices: 372 us -> 127 us
  starting transfers between devices: 0.5 us -> 58.6 us
  blocking collectives: 0 us -> 14.4 us
  local copies, waits for them, and re-layouts: 20.2 us -> 30.1 us
  other arithmetic: 10.4 us -> 18.5 us
    all_gather x4 -> x1, waiting for transfers between devices: 171 us -> 0.01 us  [local(): gate_all = lax.all_gather(gate_grad, 'row', axis=0, tiled=True)]
    ppermute x0 -> x14, waiting for transfers between devices: none -> 98.9 us  [shift_row(): return lax.ppermute(x, 'row', [(i, (i + step) % ROWS) for i in range(ROWS)])]
    psum x1 -> x0, waiting for transfers between devices: 88.9 us -> none  [local(): lax.psum(partial_grad.astype(jnp.bfloat16), 'row').astype(jnp.float32)]
    unnamed x10 -> x2, waiting for transfers between devices: 78.7 us -> 0.03 us
    all_to_all x0 -> x7, starting transfers between devices: none -> 34.5 us  [exchange(): return lax.all_to_all(x, axis, 0, 0, axis_index_groups=groups, tiled=True)]
    reduce_scatter x1, waiting for transfers between devices: 33.5 us -> 7.33 us  [local(): lax.psum_scatter(partial, 'row', scatter_dimension=0, tiled=True)]
    ppermute x0 -> x14, starting transfers between devices: none -> 24.1 us  [shift_row(): return lax.ppermute(x, 'row', [(i, (i + step) % ROWS) for i in range(ROWS)])]
    all_to_all x0 -> x7, waiting for transfers between devices: none -> 21 us  [exchange(): return lax.all_to_all(x, axis, 0, 0, axis_index_groups=groups, tiled=True)]
  transfers between devices with their start and end apart: 8 -> 23, of which waited for: 8 -> 15; matrix products, arithmetic and copies ran while one was open for 13% -> 22% of each run, Pallas kernels for 0% -> 0%
where the time goes in v1:
time: 296 us; the launch traced here: 294 us
  waiting for transfers between devices  127 us (43%)
  starting transfers between devices  58.6 us (20%)
  matrix products  30.3 us (10%)
  local copies, waits for them, and re-layouts  30.1 us (10%)
  other arithmetic  18.5 us (6%)
  blocking collectives  14.4 us (5%)
  between operations  14.3 us (5%)
    ppermute x14, waiting for transfers between devices, shift_row(): return lax.ppermute(x, 'row', [(i, (i + step) % ROWS) for i in range(ROWS)])  98.9 us
    all_to_all x7, starting transfers between devices, exchange(): return lax.all_to_all(x, axis, 0, 0, axis_index_groups=groups, tiled=True)  34.5 us
    ppermute x14, starting transfers between devices, shift_row(): return lax.ppermute(x, 'row', [(i, (i + step) % ROWS) for i in range(ROWS)])  24.1 us
    all_to_all x7, waiting for transfers between devices, exchange(): return lax.all_to_all(x, axis, 0, 0, axis_index_groups=groups, tiled=True)  21 us
    unnamed x51, local copies, waits for them, and re-layouts  15.3 us
    all_to_all x2, blocking collectives, exchange(): return lax.all_to_all(x, axis, 0, 0, axis_index_groups=groups, tiled=True)  14.4 us
    dot_general x3, matrix products, contract_tokens(): lax.dot_general(left, right, (((0,), (0,)), ((), ())), preferred_element_...  12.7 us
    reduce_scatter x1, waiting for transfers between devices, local(): lax.psum_scatter(partial, 'row', scatter_dimension=0, tiled=True)  7.33 us
  transfers between devices with their start and end apart: 23, of which 15 were waited for; matrix products, arithmetic and copies ran while one was open for 22% of the time, Pallas kernels for 0%

profile of v1, /device:TPU:8, one launch (start us, length us, event | category | flops | bytes accessed | tf_op | source)
XLA Modules:
  0.0 293.5 jit_solution(5786018607788384870)
XLA Ops:
  7.2 2.1 broadcast_in_dim.6
  9.3 6.3 %all-to-all-start = ((bf16[8,128,512]{2,1,0:T(8,128)(2,1)}), bf16[8,128,512]{2,1,0:T(8,128)(2,1)}, u32[]{:S(2)}, u32[]{:S(2)}) async-start(bf16[8,128,512]{2,1,0:T(8,128)(2,1)} %broadcast_in_dim.6), calls=%async_computation | async-start | bytes 2097152 | tf_op jit(solution)/shard_map/all_to_all | solution.py:16
  15.6 1.4 fusion.7
  17.1 5.5 %collective-permute-start = (bf16[128,1792]{1,0:T(8,128)(2,1)S(1)}, bf16[128,1792]{1,0:T(8,128)(2,1)S(1)}, u32[]{:S(2)}, u32[]{:S(2)}) collective-permute-start(bf16[128,1792]{1,0:T(8,128)(2,1)S(1)} %fusion.7), channel_id=1, source_target_pairs={{0,56},{8,0},{16,8},{24,16},{32,24},{40,32},{48,40},{56,48},{1,57}... | collective-permute-start | bytes 1376264 | tf_op jit(solution)/shard_map/ppermute | solution.py:12
  22.5 9.2 %collective-permute-done = bf16[128,1792]{1,0:T(8,128)(2,1)S(1)} collective-permute-done((bf16[128,1792]{1,0:T(8,128)(2,1)S(1)}, bf16[128,1792]{1,0:T(8,128)(2,1)S(1)}, u32[]{:S(2)}, u32[]{:S(2)}) %collective-permute-start) | collective-permute-done | bytes 458784 | tf_op jit(solution)/shard_map/ppermute | solution.py:12
  32.5 2.7 collective-permute-done.1
  35.3 5.1 %convolution_convert_fusion = bf16[1024,1792]{1,0:T(8,128)(2,1)} fusion(bf16[1024,512]{1,0:T(8,128)(2,1)} %bitcast, bf16[512,1792]{1,0:T(8,128)(2,1)S(1)} %copy-done), kind=kOutput, calls=%fused_computation.2 | convolution fusion | flops 1880883200 | bytes 6553600 | tf_op jit(solution)/shard_map/dot_general | solution.py:66
  40.5 3.2 %collective-permute-start.2 = (bf16[128,1792]{1,0:T(8,128)(2,1)}, bf16[128,1792]{1,0:T(8,128)(2,1)S(1)}, u32[]{:S(2)}, u32[]{:S(2)}) collective-permute-start(bf16[128,1792]{1,0:T(8,128)(2,1)} %copy-done.8), channel_id=1, source_target_pairs={{0,56},{8,0},{16,8},{24,16},{32,24},{40,32},{48,40},{56,48},{1,57}... | collective-permute-start | bytes 1376264 | tf_op jit(solution)/shard_map/ppermute | solution.py:12
  43.8 8.7 %collective-permute-done.4 = bf16[128,1792]{1,0:T(8,128)(2,1)S(1)} collective-permute-done((bf16[128,1792]{1,0:T(8,128)(2,1)}, bf16[128,1792]{1,0:T(8,128)(2,1)S(1)}, u32[]{:S(2)}, u32[]{:S(2)}) %collective-permute-start.4) | collective-permute-done | bytes 458784 | tf_op jit(solution)/shard_map/ppermute | solution.py:12
  53.2 6.0 %collective-permute-done.2 = bf16[128,1792]{1,0:T(8,128)(2,1)S(1)} collective-permute-done((bf16[128,1792]{1,0:T(8,128)(2,1)}, bf16[128,1792]{1,0:T(8,128)(2,1)S(1)}, u32[]{:S(2)}, u32[]{:S(2)}) %collective-permute-start.2) | collective-permute-done | bytes 458784 | tf_op jit(solution)/shard_map/ppermute | solution.py:12
  59.2 3.6 %collective-permute-start.3 = (bf16[128,1792]{1,0:T(8,128)(2,1)S(1)}, bf16[128,1792]{1,0:T(8,128)(2,1)S(1)}, u32[]{:S(2)}, u32[]{:S(2)}) collective-permute-start(bf16[128,1792]{1,0:T(8,128)(2,1)S(1)} %collective-permute-done.2), channel_id=1, source_target_pairs={{0,56},{8,0},{16,8},{24,16},{32,24},{40,32},{48,40},{56,48},{1,57}... | collective-permute-start | bytes 1376264 | tf_op jit(solution)/shard_map/ppermute | solution.py:12
  62.8 13.5 %collective-permute-done.5 = bf16[128,1792]{1,0:T(8,128)(2,1)S(1)} collective-permute-done((bf16[128,1792]{1,0:T(8,128)(2,1)S(1)}, bf16[128,1792]{1,0:T(8,128)(2,1)S(1)}, u32[]{:S(2)}, u32[]{:S(2)}) %collective-permute-start.5) | collective-permute-done | bytes 458784 | tf_op jit(solution)/shard_map/ppermute | solution.py:12
  77.1 3.6 %collective-permute-done.3 = bf16[128,1792]{1,0:T(8,128)(2,1)S(1)} collective-permute-done((bf16[128,1792]{1,0:T(8,128)(2,1)S(1)}, bf16[128,1792]{1,0:T(8,128)(2,1)S(1)}, u32[]{:S(2)}, u32[]{:S(2)}) %collective-permute-start.3) | collective-permute-done | bytes 458784 | tf_op jit(solution)/shard_map/ppermute | solution.py:12
  81.4 18.8 %collective-permute-done.6 = bf16[128,1792]{1,0:T(8,128)(2,1)} collective-permute-done((bf16[128,1792]{1,0:T(8,128)(2,1)S(1)}, bf16[128,1792]{1,0:T(8,128)(2,1)}, u32[]{:S(2)}, u32[]{:S(2)}) %collective-permute-start.6) | collective-permute-done | bytes 458784 | tf_op jit(solution)/shard_map/ppermute | solution.py:12
  100.2 7.3 %reduce-scatter.2.cloned.1.call-done = bf16[128,1792]{1,0:T(8,128)(2,1)} async-done(((bf16[1024,1792]{1,0:T(8,128)(2,1)}), bf16[128,1792]{1,0:T(8,128)(2,1)}) %reduce-scatter.2.cloned.1.call-update) | async-done | bytes 458768 | tf_op jit(solution)/shard_map/reduce_scatter | solution.py:68
  107.6 2.2 fusion.10
  109.8 2.2 constant_dynamic-update-slice_fusion.7
  112.0 0.9 collective-permute-start.7
  113.0 1.1 collective-permute-start.11
  114.1 1.1 constant_dynamic-update-slice_fusion.14
  115.2 1.1 constant_dynamic-update-slice_fusion.11
  116.3 1.1 constant_dynamic-update-slice_fusion.10
  117.4 1.1 constant_dynamic-update-slice_fusion.8
  118.4 9.8 %collective-permute-done.7 = bf16[128,1792]{1,0:T(8,128)(2,1)S(1)} collective-permute-done((bf16[128,1792]{1,0:T(8,128)(2,1)S(1)}, bf16[128,1792]{1,0:T(8,128)(2,1)S(1)}, u32[]{:S(2)}, u32[]{:S(2)}) %collective-permute-start.7) | collective-permute-done | bytes 458784 | tf_op jit(solution)/shard_map/ppermute | solution.py:12
  128.2 2.5 collective-permute-start.8
  130.7 3.6 %convolution_convert_fusion.1 = bf16[512,1792]{1,0:T(8,128)(2,1)S(1)} fusion(bf16[1024,1792]{1,0:T(8,128)(2,1)S(1)} %constant_dynamic-update-slice_fusion.8, s32[]{:T(128)S(6)} %select_n.8, bf16[1024,512]{1,0:T(8,128)(2,1)} %bitcast), kind=kOutput, calls=%fused_computation.3 | convolution fusion | flops 1882062848 | bytes 6553604 | tf_op jit(solution)/shard_map/dot_general | solution.py:44
  134.3 1.4 copy.24
  135.7 4.8 %all-to-all-start.7 = ((bf16[2,2,128,1792]{3,2,1,0:T(8,128)(2,1)}), bf16[2,2,128,1792]{3,2,1,0:T(8,128)(2,1)}, u32[]{:S(2)}, u32[]{:S(2)}) async-start(bf16[2,2,128,1792]{3,2,1,0:T(8,128)(2,1)} %bitcast.41), calls=%async_computation.8 | async-start | bytes 3670016 | tf_op jit(solution)/shard_map/all_to_all | solution.py:16
  140.6 9.9 %collective-permute-done.8 = bf16[128,1792]{1,0:T(8,128)(2,1)} collective-permute-done((bf16[128,1792]{1,0:T(8,128)(2,1)S(1)}, bf16[128,1792]{1,0:T(8,128)(2,1)}, u32[]{:S(2)}, u32[]{:S(2)}) %collective-permute-start.8) | collective-permute-done | bytes 458784 | tf_op jit(solution)/shard_map/ppermute | solution.py:12
  150.5 3.4 %collective-permute-start.9 = (bf16[128,1792]{1,0:T(8,128)(2,1)}, bf16[128,1792]{1,0:T(8,128)(2,1)}, u32[]{:S(2)}, u32[]{:S(2)}) collective-permute-start(bf16[128,1792]{1,0:T(8,128)(2,1)} %collective-permute-done.8), channel_id=1, source_target_pairs={{0,56},{8,0},{16,8},{24,16},{32,24},{40,32},{48,40},{56,48},{1,57}... | collective-permute-start | bytes 1376264 | tf_op jit(solution)/shard_map/ppermute | solution.py:12
  153.9 1.1 broadcast_in_dim.7
  155.0 5.8 %all-to-all-start.2 = ((bf16[8,128,512]{2,1,0:T(8,128)(2,1)}), bf16[8,128,512]{2,1,0:T(8,128)(2,1)S(1)}, u32[]{:S(2)}, u32[]{:S(2)}) async-start(bf16[8,128,512]{2,1,0:T(8,128)(2,1)} %broadcast_in_dim.7), calls=%async_computation.3 | async-start | bytes 2097152 | tf_op jit(solution)/shard_map/all_to_all | solution.py:16
  160.8 2.6 fusion.19
  164.2 9.3 %collective-permute-done.9 = bf16[128,1792]{1,0:T(8,128)(2,1)} collective-permute-done((bf16[128,1792]{1,0:T(8,128)(2,1)}, bf16[128,1792]{1,0:T(8,128)(2,1)}, u32[]{:S(2)}, u32[]{:S(2)}) %collective-permute-start.9) | collective-permute-done | bytes 458784 | tf_op jit(solution)/shard_map/ppermute | solution.py:12
  173.5 3.7 %collective-permute-start.10 = (bf16[128,1792]{1,0:T(8,128)(2,1)}, bf16[128,1792]{1,0:T(8,128)(2,1)S(1)}, u32[]{:S(2)}, u32[]{:S(2)}) collective-permute-start(bf16[128,1792]{1,0:T(8,128)(2,1)} %collective-permute-done.9), channel_id=1, source_target_pairs={{0,56},{8,0},{16,8},{24,16},{32,24},{40,32},{48,40},{56,48},{1,57}... | collective-permute-start | bytes 1376264 | tf_op jit(solution)/shard_map/ppermute | solution.py:12
  177.2 1.8 constant_dynamic-update-slice_fusion.5
  179.1 1.8 constant_dynamic-update-slice_fusion.4
  180.9 7.4 %collective-permute-done.10 = bf16[128,1792]{1,0:T(8,128)(2,1)S(1)} collective-permute-done((bf16[128,1792]{1,0:T(8,128)(2,1)}, bf16[128,1792]{1,0:T(8,128)(2,1)S(1)}, u32[]{:S(2)}, u32[]{:S(2)}) %collective-permute-start.10) | collective-permute-done | bytes 458784 | tf_op jit(solution)/shard_map/ppermute | solution.py:12
  188.2 0.8 constant_dynamic-update-slice_fusion.3
  189.1 0.8 constant_dynamic-update-slice_fusion.2
  189.9 1.8 constant_dynamic-update-slice_fusion.1
  191.7 1.8 constant_dynamic-update-slice_fusion
  193.5 4.7 %convolution_convert_fusion.2 = bf16[1792,512]{1,0:T(8,128)(2,1)S(1)} fusion(bf16[1024,1792]{1,0:T(8,128)(2,1)} %constant_dynamic-update-slice_fusion, s32[]{:T(128)S(6)} %select_n.8, bf16[1024,512]{1,0:T(8,128)(2,1)S(1)} %bitcast.47), kind=kOutput, calls=%fused_computation.4 | convolution fusion | flops 1882062848 | bytes 6553604 | tf_op jit(solution)/shard_map/dot_general | solution.py:44
  198.4 6.1 %all_to_all.45 = bf16[2,2,448,512]{3,2,1,0:T(8,128)(2,1)} all-to-all(bf16[2,2,448,512]{3,2,1,0:T(8,128)(2,1)S(1)} %bitcast.42), channel_id=1, replica_groups={{0,64},{128,192},{1,65},{129,193},{2,66},{130,194},{3,67},{131,195},{4,..., dimensions={0} | all-to-all | bytes 3670016 | tf_op jit(solution)/shard_map/all_to_all | solution.py:16
  204.5 4.2 %all-to-all-start.8 = ((bf16[2,128,1792]{2,1,0:T(8,128)(2,1)}), bf16[2,128,1792]{2,1,0:T(8,128)(2,1)S(1)}, u32[]{:S(2)}, u32[]{:S(2)}) async-start(bf16[2,128,1792]{2,1,0:T(8,128)(2,1)} %fusion.19), calls=%async_computation.9 | async-start | bytes 1835008 | tf_op jit(solution)/shard_map/all_to_all | solution.py:16
  208.7 2.6 fusion.18
  211.3 5.9 %copy.17 = bf16[1792,1024]{1,0:T(8,128)(2,1)} copy(bf16[1792,1024]{0,1:T(8,128)(2,1)} %bitcast.43) | data formatting | bytes 7340032 | tf_op jit(solution)/shard_map/dot_general | solution.py:44
  217.2 4.4 %convert_bitcast_fusion = bf16[2,2,448,512]{3,2,0,1:T(8,128)(2,1)S(1)} fusion(bf16[2,2,448,1024]{3,2,1,0:T(8,128)(2,1)} %bitcast.44, bf16[1024,512,1,1]{1,0,3,2:T(8,128)(2,1)} %bitcast.48), kind=kOutput, calls=%fused_computation.17 | convolution fusion | flops 1879965696 | bytes 6553600 | tf_op jit(solution)/shard_map/dot_general | solution.py:44
  221.6 1.4 copy.18
  223.1 8.3 %all_to_all.46 = bf16[2,2,448,512]{3,2,1,0:T(8,128)(2,1)} all-to-all(bf16[2,2,448,512]{3,2,1,0:T(8,128)(2,1)} %copy.18), channel_id=1, replica_groups={{0,64},{128,192},{1,65},{129,193},{2,66},{130,194},{3,67},{131,195},{4,..., dimensions={0} | all-to-all | bytes 3670016 | tf_op jit(solution)/shard_map/all_to_all | solution.py:16
  231.3 4.8 %all-to-all-start.6 = ((bf16[2,448,512]{2,1,0:T(8,128)(2,1)}), bf16[2,448,512]{2,1,0:T(8,128)(2,1)}, u32[]{:S(2)}, u32[]{:S(2)}) async-start(bf16[2,448,512]{2,1,0:T(8,128)(2,1)} %fusion.18), calls=%async_computation.7 | async-start | bytes 1835008 | tf_op jit(solution)/shard_map/all_to_all | solution.py:16
  236.1 6.2 %fusion.25 = f32[1024,512]{1,0:T(8,128)} fusion(bf16[1024,1792]{1,0:T(8,128)(2,1)} %constant_dynamic-update-slice_fusion, bf16[1792,512]{1,0:T(8,128)(2,1)} %param.12), kind=kOutput, calls=%fused_computation.62 | convolution fusion | flops 1879048192 | bytes 7602176 | tf_op jit(solution)/shard_map/dot_general | solution.py:85
  242.3 1.2 fusion.17
  243.5 7.1 %all-to-all-done.6 = bf16[2,448,512]{2,1,0:T(8,128)(2,1)} async-done(((bf16[2,448,512]{2,1,0:T(8,128)(2,1)}), bf16[2,448,512]{2,1,0:T(8,128)(2,1)}, u32[]{:S(2)}, u32[]{:S(2)}) %all-to-all-start.6) | async-done | bytes 917536 | tf_op jit(solution)/shard_map/all_to_all | solution.py:16
  250.6 3.6 %all-to-all-start.4 = ((bf16[2,448,512]{2,1,0:T(8,128)(2,1)}), bf16[2,448,512]{2,1,0:T(8,128)(2,1)S(1)}, u32[]{:S(2)}, u32[]{:S(2)}) async-start(bf16[2,448,512]{2,1,0:T(8,128)(2,1)} %fusion.17), calls=%async_computation.5 | async-start | bytes 1835008 | tf_op jit(solution)/shard_map/all_to_all | solution.py:16
  254.2 6.3 %fusion.2 = bf16[1024,512]{1,0:T(8,128)(2,1)} fusion(s32[]{:T(128)S(6)} %select_n.7, f32[1024,512]{1,0:T(8,128)} %fusion.25, bf16[1024,1792]{1,0:T(8,128)(2,1)} %all-gather.2.cloned.1.call-done, bf16[1792,512]{1,0:T(8,128)(2,1)} %param.11), kind=kOutput, calls=%fused_computation.7 | convolution fusion | flops 1880621056 | bytes 8650756 | tf_op jit(solution)/shard_map/dot_general | solution.py:86
  260.5 7.2 %all-to-all-done.4 = bf16[2,448,512]{2,1,0:T(8,128)(2,1)S(1)} async-done(((bf16[2,448,512]{2,1,0:T(8,128)(2,1)}), bf16[2,448,512]{2,1,0:T(8,128)(2,1)S(1)}, u32[]{:S(2)}, u32[]{:S(2)}) %all-to-all-start.4) | async-done | bytes 917536 | tf_op jit(solution)/shard_map/all_to_all | solution.py:16
  267.7 0.9 copy-done.4
  268.6 5.0 %all-to-all-start.1 = ((bf16[8,128,512]{2,1,0:T(8,128)(2,1)}), bf16[8,128,512]{2,1,0:T(8,128)(2,1)S(1)}, u32[]{:S(2)}, u32[]{:S(2)}) async-start(bf16[8,128,512]{2,1,0:T(8,128)(2,1)} %bitcast.49), calls=%async_computation.2 | async-start | bytes 2097152 | tf_op jit(solution)/shard_map/all_to_all | solution.py:16
  273.6 2.3 add_bitcast_fusion
  275.9 2.2 add_bitcast_fusion.1
  278.1 1.1 add_bitcast_fusion.2
  279.1 6.7 %all-to-all-done.1 = bf16[8,128,512]{2,1,0:T(8,128)(2,1)S(1)} async-done(((bf16[8,128,512]{2,1,0:T(8,128)(2,1)}), bf16[8,128,512]{2,1,0:T(8,128)(2,1)S(1)}, u32[]{:S(2)}, u32[]{:S(2)}) %all-to-all-start.1) | async-done | bytes 1048608 | tf_op jit(solution)/shard_map/all_to_all | solution.py:16
  285.9 0.8 reduce_sum.12
  (61 shorter events, 4.5 us)
Async XLA Ops:
  7.2 28.1 %copy-start = (bf16[512,1792]{1,0:T(8,128)(2,1)S(1)}, bf16[512,1792]{1,0:T(8,128)(2,1)}, u32[]{:S(2)}) copy-start(bf16[512,1792]{1,0:T(8,128)(2,1)} %param.13) | copy-start | bytes 5505028
  9.3 26.0 %all-to-all-start = ((bf16[8,128,512]{2,1,0:T(8,128)(2,1)}), bf16[8,128,512]{2,1,0:T(8,128)(2,1)}, u32[]{:S(2)}, u32[]{:S(2)}) async-start(bf16[8,128,512]{2,1,0:T(8,128)(2,1)} %broadcast_in_dim.6), calls=%async_computation | async-start | bytes 2097152 | tf_op jit(solution)/shard_map/all_to_all | solution.py:16
  15.6 92.0 %reduce-scatter.2.cloned.1.call-start = ((), (), s32[]{:S(2)}) async-start(), calls=%async_computation.10 | async-start | bytes 4128768 | tf_op jit(solution)/shard_map/reduce_scatter | solution.py:68
  17.1 14.7 %collective-permute-start = (bf16[128,1792]{1,0:T(8,128)(2,1)S(1)}, bf16[128,1792]{1,0:T(8,128)(2,1)S(1)}, u32[]{:S(2)}, u32[]{:S(2)}) collective-permute-start(bf16[128,1792]{1,0:T(8,128)(2,1)S(1)} %fusion.7), channel_id=1, source_target_pairs={{0,56},{8,0},{16,8},{24,16},{32,24},{40,32},{48,40},{56,48},{1,57}... | collective-permute-start | bytes 1376264 | tf_op jit(solution)/shard_map/ppermute | solution.py:12
  22.5 12.7 %collective-permute-start.1 = (bf16[128,1792]{1,0:T(8,128)(2,1)S(1)}, bf16[128,1792]{1,0:T(8,128)(2,1)}, u32[]{:S(2)}, u32[]{:S(2)}) collective-permute-start(bf16[128,1792]{1,0:T(8,128)(2,1)S(1)} %fusion.7), channel_id=1, source_target_pairs={{0,8},{8,16},{16,24},{24,32},{32,40},{40,48},{48,56},{56,0},{1,9},... | collective-permute-start | bytes 1376264 | tf_op jit(solution)/shard_map/ppermute | solution.py:12
  31.7 0.8 copy-start.8
  40.4 67.2 %copy-start.2 = (bf16[128,1792]{1,0:T(8,128)(2,1)S(1)}, bf16[128,1792]{1,0:T(8,128)(2,1)}, u32[]{:S(2)}) copy-start(bf16[128,1792]{1,0:T(8,128)(2,1)} %param.9) | copy-start | bytes 1376260
  40.4 67.2 %copy-start.6 = (bf16[128,1792]{1,0:T(8,128)(2,1)S(1)}, bf16[128,1792]{1,0:T(8,128)(2,1)}, u32[]{:S(2)}) copy-start(bf16[128,1792]{1,0:T(8,128)(2,1)} %param.10) | copy-start | bytes 1376260
  40.4 170.9 %all-gather.2.cloned.1.call-start = ((), (), s32[]{:S(2)}) async-start(), calls=%async_computation.11 | async-start | bytes 4128768 | tf_op jit(solution)/shard_map/all_gather | solution.py:75
  40.5 12.0 %collective-permute-start.4 = (bf16[128,1792]{1,0:T(8,128)(2,1)}, bf16[128,1792]{1,0:T(8,128)(2,1)S(1)}, u32[]{:S(2)}, u32[]{:S(2)}) collective-permute-start(bf16[128,1792]{1,0:T(8,128)(2,1)} %collective-permute-done.1), channel_id=1, source_target_pairs={{0,8},{8,16},{16,24},{24,32},{32,40},{40,48},{48,56},{56,0},{1,9},... | collective-permute-start | bytes 1376264 | tf_op jit(solution)/shard_map/ppermute | solution.py:12
  40.5 18.7 %collective-permute-start.2 = (bf16[128,1792]{1,0:T(8,128)(2,1)}, bf16[128,1792]{1,0:T(8,128)(2,1)S(1)}, u32[]{:S(2)}, u32[]{:S(2)}) collective-permute-start(bf16[128,1792]{1,0:T(8,128)(2,1)} %copy-done.8), channel_id=1, source_target_pairs={{0,56},{8,0},{16,8},{24,16},{32,24},{40,32},{48,40},{56,48},{1,57}... | collective-permute-start | bytes 1376264 | tf_op jit(solution)/shard_map/ppermute | solution.py:12
  52.4 0.8 copy-start.9
  53.2 23.1 %collective-permute-start.5 = (bf16[128,1792]{1,0:T(8,128)(2,1)S(1)}, bf16[128,1792]{1,0:T(8,128)(2,1)S(1)}, u32[]{:S(2)}, u32[]{:S(2)}) collective-permute-start(bf16[128,1792]{1,0:T(8,128)(2,1)S(1)} %collective-permute-done.4), channel_id=1, source_target_pairs={{0,8},{8,16},{16,24},{24,32},{32,40},{40,48},{48,56},{56,0},{1,9},... | collective-permute-start | bytes 1376264 | tf_op jit(solution)/shard_map/ppermute | solution.py:12
  59.2 17.9 %copy-start.12 = (bf16[128,1792]{1,0:T(8,128)(2,1)}, bf16[128,1792]{1,0:T(8,128)(2,1)S(1)}, u32[]{:S(2)}) copy-start(bf16[128,1792]{1,0:T(8,128)(2,1)S(1)} %collective-permute-done.2) | copy-start | bytes 1376260
  59.2 21.4 %collective-permute-start.3 = (bf16[128,1792]{1,0:T(8,128)(2,1)S(1)}, bf16[128,1792]{1,0:T(8,128)(2,1)S(1)}, u32[]{:S(2)}, u32[]{:S(2)}) collective-permute-start(bf16[128,1792]{1,0:T(8,128)(2,1)S(1)} %collective-permute-done.2), channel_id=1, source_target_pairs={{0,56},{8,0},{16,8},{24,16},{32,24},{40,32},{48,40},{56,48},{1,57}... | collective-permute-start | bytes 1376264 | tf_op jit(solution)/shard_map/ppermute | solution.py:12
  76.3 0.8 copy-start.11
  77.1 23.2 %collective-permute-start.6 = (bf16[128,1792]{1,0:T(8,128)(2,1)S(1)}, bf16[128,1792]{1,0:T(8,128)(2,1)}, u32[]{:S(2)}, u32[]{:S(2)}) collective-permute-start(bf16[128,1792]{1,0:T(8,128)(2,1)S(1)} %collective-permute-done.5), channel_id=1, source_target_pairs={{0,8},{8,16},{16,24},{24,32},{32,40},{40,48},{48,56},{56,0},{1,9},... | collective-permute-start | bytes 1376264 | tf_op jit(solution)/shard_map/ppermute | solution.py:12
  80.6 0.8 copy-start.14
  109.8 5.3 %copy-start.13 = (bf16[128,1792]{1,0:T(8,128)(2,1)S(1)}, bf16[128,1792]{1,0:T(8,128)(2,1)}, u32[]{:S(2)}) copy-start(bf16[128,1792]{1,0:T(8,128)(2,1)} %copy-done.12) | copy-start | bytes 1376260
  109.8 5.4 %copy-start.15 = (bf16[128,1792]{1,0:T(8,128)(2,1)S(1)}, bf16[128,1792]{1,0:T(8,128)(2,1)}, u32[]{:S(2)}) copy-start(bf16[128,1792]{1,0:T(8,128)(2,1)} %copy-done.14) | copy-start | bytes 1376260
  109.8 7.5 %copy-start.10 = (bf16[128,1792]{1,0:T(8,128)(2,1)S(1)}, bf16[128,1792]{1,0:T(8,128)(2,1)}, u32[]{:S(2)}) copy-start(bf16[128,1792]{1,0:T(8,128)(2,1)} %copy-done.9) | copy-start | bytes 1376260
  112.0 16.2 %collective-permute-start.7 = (bf16[128,1792]{1,0:T(8,128)(2,1)S(1)}, bf16[128,1792]{1,0:T(8,128)(2,1)S(1)}, u32[]{:S(2)}, u32[]{:S(2)}) collective-permute-start(bf16[128,1792]{1,0:T(8,128)(2,1)S(1)} %get-tuple-element.33), channel_id=1, source_target_pairs={{0,56},{8,0},{16,8},{24,16},{32,24},{40,32},{48,40},{56,48},{1,57}... | collective-permute-start | bytes 1376264 | tf_op jit(solution)/shard_map/ppermute | solution.py:12
  113.0 27.5 %collective-permute-start.11 = (bf16[128,1792]{1,0:T(8,128)(2,1)S(1)}, bf16[128,1792]{1,0:T(8,128)(2,1)}, u32[]{:S(2)}, u32[]{:S(2)}) collective-permute-start(bf16[128,1792]{1,0:T(8,128)(2,1)S(1)} %get-tuple-element.33), channel_id=1, source_target_pairs={{0,8},{8,16},{16,24},{24,32},{32,40},{40,48},{48,56},{56,0},{1,9},... | collective-permute-start | bytes 1376264 | tf_op jit(solution)/shard_map/ppermute | solution.py:12
  128.2 6.1 %copy-start.16 = (bf16[128,1792]{1,0:T(8,128)(2,1)}, bf16[128,1792]{1,0:T(8,128)(2,1)S(1)}, u32[]{:S(2)}) copy-start(bf16[128,1792]{1,0:T(8,128)(2,1)S(1)} %collective-permute-done.7) | copy-start | bytes 1376260
  128.2 22.3 %collective-permute-start.8 = (bf16[128,1792]{1,0:T(8,128)(2,1)S(1)}, bf16[128,1792]{1,0:T(8,128)(2,1)}, u32[]{:S(2)}, u32[]{:S(2)}) collective-permute-start(bf16[128,1792]{1,0:T(8,128)(2,1)S(1)} %collective-permute-done.7), channel_id=1, source_target_pairs={{0,56},{8,0},{16,8},{24,16},{32,24},{40,32},{48,40},{56,48},{1,57}... | collective-permute-start | bytes 1376264 | tf_op jit(solution)/shard_map/ppermute | solution.py:12
  134.3 19.6 %copy-start.18 = (bf16[128,512]{1,0:T(8,128)(2,1)S(1)}, bf16[128,512]{1,0:T(8,128)(2,1)}, u32[]{:S(2)}) copy-start(bf16[128,512]{1,0:T(8,128)(2,1)} %param.7) | copy-start | bytes 393220
  135.7 18.3 %all-to-all-start.7 = ((bf16[2,2,128,1792]{3,2,1,0:T(8,128)(2,1)}), bf16[2,2,128,1792]{3,2,1,0:T(8,128)(2,1)}, u32[]{:S(2)}, u32[]{:S(2)}) async-start(bf16[2,2,128,1792]{3,2,1,0:T(8,128)(2,1)} %bitcast.41), calls=%async_computation.8 | async-start | bytes 3670016 | tf_op jit(solution)/shard_map/all_to_all | solution.py:16
  140.5 22.9 %copy-start.17 = (bf16[128,1792]{1,0:T(8,128)(2,1)S(1)}, bf16[128,1792]{1,0:T(8,128)(2,1)}, u32[]{:S(2)}) copy-start(bf16[128,1792]{1,0:T(8,128)(2,1)} %copy-done.16) | copy-start | bytes 1376260
  140.5 23.7 %collective-permute-start.12 = (bf16[128,1792]{1,0:T(8,128)(2,1)}, bf16[128,1792]{1,0:T(8,128)(2,1)}, u32[]{:S(2)}, u32[]{:S(2)}) collective-permute-start(bf16[128,1792]{1,0:T(8,128)(2,1)} %collective-permute-done.11), channel_id=1, source_target_pairs={{0,8},{8,16},{16,24},{24,32},{32,40},{40,48},{48,56},{56,0},{1,9},... | collective-permute-start | bytes 1376264 | tf_op jit(solution)/shard_map/ppermute | solution.py:12
  150.5 23.0 %collective-permute-start.9 = (bf16[128,1792]{1,0:T(8,128)(2,1)}, bf16[128,1792]{1,0:T(8,128)(2,1)}, u32[]{:S(2)}, u32[]{:S(2)}) collective-permute-start(bf16[128,1792]{1,0:T(8,128)(2,1)} %collective-permute-done.8), channel_id=1, source_target_pairs={{0,56},{8,0},{16,8},{24,16},{32,24},{40,32},{48,40},{56,48},{1,57}... | collective-permute-start | bytes 1376264 | tf_op jit(solution)/shard_map/ppermute | solution.py:12
  155.0 38.5 %all-to-all-start.2 = ((bf16[8,128,512]{2,1,0:T(8,128)(2,1)}), bf16[8,128,512]{2,1,0:T(8,128)(2,1)S(1)}, u32[]{:S(2)}, u32[]{:S(2)}) async-start(bf16[8,128,512]{2,1,0:T(8,128)(2,1)} %broadcast_in_dim.7), calls=%async_computation.3 | async-start | bytes 2097152 | tf_op jit(solution)/shard_map/all_to_all | solution.py:16
  164.2 24.9 %collective-permute-start.13 = (bf16[128,1792]{1,0:T(8,128)(2,1)}, bf16[128,1792]{1,0:T(8,128)(2,1)S(1)}, u32[]{:S(2)}, u32[]{:S(2)}) collective-permute-start(bf16[128,1792]{1,0:T(8,128)(2,1)} %collective-permute-done.12), channel_id=1, source_target_pairs={{0,8},{8,16},{16,24},{24,32},{32,40},{40,48},{48,56},{56,0},{1,9},... | collective-permute-start | bytes 1376264 | tf_op jit(solution)/shard_map/ppermute | solution.py:12
  173.5 14.7 %collective-permute-start.10 = (bf16[128,1792]{1,0:T(8,128)(2,1)}, bf16[128,1792]{1,0:T(8,128)(2,1)S(1)}, u32[]{:S(2)}, u32[]{:S(2)}) collective-permute-start(bf16[128,1792]{1,0:T(8,128)(2,1)} %collective-permute-done.9), channel_id=1, source_target_pairs={{0,56},{8,0},{16,8},{24,16},{32,24},{40,32},{48,40},{56,48},{1,57}... | collective-permute-start | bytes 1376264 | tf_op jit(solution)/shard_map/ppermute | solution.py:12
  193.5 4.7 %copy-start.7 = (bf16[8,128,512]{2,1,0:T(8,128)(2,1)}, bf16[8,128,512]{2,1,0:T(8,128)(2,1)S(1)}, u32[]{:S(2)}) copy-start(bf16[8,128,512]{2,1,0:T(8,128)(2,1)S(1)} %all-to-all-done.2) | copy-start | bytes 3145732
  204.5 18.5 %all-to-all-start.8 = ((bf16[2,128,1792]{2,1,0:T(8,128)(2,1)}), bf16[2,128,1792]{2,1,0:T(8,128)(2,1)S(1)}, u32[]{:S(2)}, u32[]{:S(2)}) async-start(bf16[2,128,1792]{2,1,0:T(8,128)(2,1)} %fusion.19), calls=%async_computation.9 | async-start | bytes 1835008 | tf_op jit(solution)/shard_map/all_to_all | solution.py:16
  223.1 19.3 %copy-start.3 = (bf16[2,128,1792]{2,1,0:T(8,128)(2,1)}, bf16[2,128,1792]{2,1,0:T(8,128)(2,1)S(1)}, u32[]{:S(2)}) copy-start(bf16[2,128,1792]{2,1,0:T(8,128)(2,1)S(1)} %all-to-all-done.8) | copy-start | bytes 2752516
  231.3 19.3 %all-to-all-start.6 = ((bf16[2,448,512]{2,1,0:T(8,128)(2,1)}), bf16[2,448,512]{2,1,0:T(8,128)(2,1)}, u32[]{:S(2)}, u32[]{:S(2)}) async-start(bf16[2,448,512]{2,1,0:T(8,128)(2,1)} %fusion.18), calls=%async_computation.7 | async-start | bytes 1835008 | tf_op jit(solution)/shard_map/all_to_all | solution.py:16
  236.1 6.2 %copy-start.1 = (bf16[2,2,448,512]{3,2,1,0:T(8,128)(2,1)S(1)}, bf16[2,2,448,512]{3,2,1,0:T(8,128)(2,1)}, u32[]{:S(2)}) copy-start(bf16[2,2,448,512]{3,2,1,0:T(8,128)(2,1)} %all_to_all.46) | copy-start | bytes 5505028
  250.6 17.1 %all-to-all-start.4 = ((bf16[2,448,512]{2,1,0:T(8,128)(2,1)}), bf16[2,448,512]{2,1,0:T(8,128)(2,1)S(1)}, u32[]{:S(2)}, u32[]{:S(2)}) async-start(bf16[2,448,512]{2,1,0:T(8,128)(2,1)} %fusion.17), calls=%async_computation.5 | async-start | bytes 1835008 | tf_op jit(solution)/shard_map/all_to_all | solution.py:16
  267.7 0.9 copy-start.4
  268.6 17.3 %all-to-all-start.1 = ((bf16[8,128,512]{2,1,0:T(8,128)(2,1)}), bf16[8,128,512]{2,1,0:T(8,128)(2,1)S(1)}, u32[]{:S(2)}, u32[]{:S(2)}) async-start(bf16[8,128,512]{2,1,0:T(8,128)(2,1)} %bitcast.49), calls=%async_computation.2 | async-start | bytes 2097152 | tf_op jit(solution)/shard_map/all_to_all | solution.py:16
  273.6 4.5 %copy-start.5 = (bf16[2,448,512]{2,1,0:T(8,128)(2,1)S(1)}, bf16[2,448,512]{2,1,0:T(8,128)(2,1)}, u32[]{:S(2)}) copy-start(bf16[2,448,512]{2,1,0:T(8,128)(2,1)} %copy-done.4) | copy-start | bytes 2752516
Sparse Core Ops, SparseCore 0:
  40.5 67.0 reduce-scatter.1
  109.9 73.8 all-gather.1

commit v2 on v1

--- a/solution.py
+++ b/solution.py
@@ -20,11 +20,23 @@
     return exchange(jnp.broadcast_to(x, (8,) + x.shape), "col").reshape(-1, x.shape[-1])
 
 
-def sum_dp(x):
-    near = exchange(jnp.swapaxes(x.astype(BF16), 0, 1), "dp", [[0, 1], [2, 3]])
-    half = (near[0].astype(F32) + near[1].astype(F32)).astype(BF16)
-    far = exchange(half, "dp", [[0, 2], [1, 3]])
-    return far[0].astype(F32) + far[1].astype(F32)
+def pick(x, at, axis):
+    return lax.dynamic_index_in_dim(x, at, axis, keepdims=False)
+
+
+def halve_core(x, core):
+    other = lax.ppermute(
+        pick(x, 1 - core, 1).astype(BF16), "dp", [(0, 1), (1, 0), (2, 3), (3, 2)]
+    )
+    return pick(x, core, 1) + other.astype(F32)
+
+
+def swap_far(x):
+    return lax.ppermute(x, "dp", [(0, 2), (2, 0), (1, 3), (3, 1)])
+
+
+def swap_x(x):
+    return lax.ppermute(x, "col", [(i, (i + 4) % 8) for i in range(8)])
 
 
 def gather_row(x, sign):
@@ -46,6 +58,9 @@
 
 def local(tokens, cotangent, gate_pre, up_pre, w_gate, w_up, w_down):
     row = lax.axis_index("row")
+    dp = lax.axis_index("dp")
+    far, core = dp >> 1, dp & 1
+    x_at = lax.axis_index("col") >> 2
     block, hidden_width = gate_pre.shape
     features = w_gate.shape[1]
 
@@ -60,13 +75,14 @@
     hidden_blocks = gather_row(hidden, 1)
 
     cot = gather_col(cotangent)
-    cot, hidden_blocks[1], hidden_blocks[7] = lax.optimization_barrier(
-        (cot, hidden_blocks[1], hidden_blocks[7])
-    )
+    early = [hidden_blocks[o] for o in (1, 2, 6, 7)]
+    cot, *early = lax.optimization_barrier((cot, *early))
+    hidden_blocks[1:3], hidden_blocks[6:] = early[:2], early[2:]
     partial = jnp.dot(cot, w_down, preferred_element_type=F32).astype(BF16)
     partial, tokens = lax.optimization_barrier((partial, tokens))
+    tok = gather_col(tokens)
     hidden_grad = lax.psum_scatter(partial, "row", scatter_dimension=0, tiled=True)
-    hidden_grad, *hidden_blocks = lax.optimization_barrier((hidden_grad, *hidden_blocks))
+    hidden_grad, tok, *hidden_blocks = lax.optimization_barrier((hidden_grad, tok, *hidden_blocks))
     hidden_grad = hidden_grad.astype(F32)
     gate_grad = (
         hidden_grad * up_value * sigmoid_gate * (1.0 + gate_value * (1.0 - sigmoid_gate))
@@ -76,17 +92,29 @@
     up_all = jnp.concatenate(gather_row(up_grad, -1), axis=0)
 
     hidden_all = jnp.concatenate(hidden_blocks, axis=0)
-    grad_down = sum_dp(
-        contract_tokens(turned(cot, row), hidden_all).reshape(2, 2, block, hidden_width)
-    )
-    tok = gather_col(tokens)
-    grad_up = sum_dp(contract_tokens(up_all, turned(tok, row)).reshape(2, 2, -1, features))
-    grad_gate = sum_dp(contract_tokens(gate_all, tok).reshape(2, 2, -1, features))
+    down = contract_tokens(turned(cot, row), hidden_all)
+    down = halve_core(down.reshape(2, 2, block, hidden_width), core)
+    away = swap_far(pick(down, 1 - far, 0).astype(BF16))
+    grad_down = pick(down, far, 0) + away.astype(F32)
+
+    gate = contract_tokens(gate_all, tok).reshape(2, 2, -1, features)
+    gate = halve_core(gate, core)
+    gate_away = pick(gate, 1 - far, 0).astype(BF16)
+    up = contract_tokens(up_all, turned(tok, row)).reshape(2, 2, -1, features)
+    up = halve_core(up, core)
+    up_away = pick(up, 1 - far, 0).astype(BF16)
+
     from_up = jnp.dot(up_all, w_up, preferred_element_type=F32)
     from_gate = jnp.dot(gate_all, w_gate, preferred_element_type=F32)
     token_grad = (from_gate + turned(from_up, (ROWS - row) & 7)).astype(BF16)
-    token_grad = exchange(token_grad.reshape(8, block, features), "col")
-    d_tokens = jnp.sum(token_grad.astype(F32), axis=0).astype(BF16)
+    token_grad = jnp.swapaxes(token_grad.reshape(2, 4, block, features), 0, 1)
+    gate_away, up_away, token_grad = lax.optimization_barrier((gate_away, up_away, token_grad))
+    grad_gate = pick(gate, far, 0) + swap_far(gate_away).astype(F32)
+    grad_up = pick(up, far, 0) + swap_far(up_away).astype(F32)
+    over_y = [[a * 4 + b for b in range(4)] for a in range(2)]
+    pair = jnp.sum(exchange(token_grad, "col", over_y).astype(F32), axis=0)
+    away = swap_x(pick(pair, 1 - x_at, 0).astype(BF16))
+    d_tokens = (pick(pair, x_at, 0) + away.astype(F32)).astype(BF16)
     return (d_tokens, grad_gate, grad_up, grad_down)
 
 

time: 296 us -> 256 us (0.86)
  blocking collectives: 14.4 us -> 0 us
  starting transfers between devices: 58.6 us -> 48.8 us
  matrix products: 30.3 us -> 21.1 us
  waiting for transfers between devices: 127 us -> 123 us
    all_to_all x7 -> x3, waiting for transfers between devices: 21 us -> 0.01 us  [exchange(): return lax.all_to_all(x, axis, 0, 0, axis_index_groups=groups, tiled=True)]
    all_to_all x7 -> x3, starting transfers between devices: 34.5 us -> 16.5 us  [exchange(): return lax.all_to_all(x, axis, 0, 0, axis_index_groups=groups, tiled=True)]
    ppermute x0 -> x7, waiting for transfers between devices: none -> 14.7 us  [the longest x3 14.7 us: swap_far(): return lax.ppermute(x, 'dp', [(0, 2), (2, 0), (1, 3), (3, 1)])]
    all_to_all x2 -> x0, blocking collectives: 14.4 us -> none  [exchange(): return lax.all_to_all(x, axis, 0, 0, axis_index_groups=groups, tiled=True)]
    ppermute x0 -> x7, starting transfers between devices: none -> 8.79 us  [the longest x3 6.26 us: swap_far(): return lax.ppermute(x, 'dp', [(0, 2), (2, 0), (1, 3), (3, 1)])]
    unnamed x51 -> x55, local copies, waits for them, and re-layouts: 15.3 us -> 21.5 us
    dot_general x1 -> x0, local copies, waits for them, and re-layouts: 5.88 us -> none  [contract_tokens(): lax.dot_general(left, right, (((0,), (0,)), ((), ())), preferred_element_...]
    convert_element_type x3 -> x1, other arithmetic: 6.4 us -> 0.68 us  [local(): d_tokens = (pick(pair, x_at, 0) + away.astype(F32)).astype(BF16)]
  transfers between devices with their start and end apart: 23 -> 26, of which waited for: 15 -> 12; matrix products, arithmetic and copies ran while one was open for 22% -> 20% of each run, Pallas kernels for 0% -> 0%
where the time goes in v2:
time: 256 us
  waiting for transfers between devices  123 us (48%)
  starting transfers between devices  48.8 us (19%)
  local copies, waits for them, and re-layouts  30.4 us (12%)
  matrix products  21.1 us (8%)
  other arithmetic  17.7 us (7%)
  between operations  14.3 us (6%)
    ppermute x14, waiting for transfers between devices, shift_row(): return lax.ppermute(x, 'row', [(i, (i + step) % ROWS) for i in range(ROWS)])  96 us
    ppermute x14, starting transfers between devices, shift_row(): return lax.ppermute(x, 'row', [(i, (i + step) % ROWS) for i in range(ROWS)])  23.5 us
    unnamed x55, local copies, waits for them, and re-layouts  21.5 us
    all_to_all x3, starting transfers between devices, exchange(): return lax.all_to_all(x, axis, 0, 0, axis_index_groups=groups, tiled=True)  16.5 us
    ppermute x3, waiting for transfers between devices, swap_far(): return lax.ppermute(x, 'dp', [(0, 2), (2, 0), (1, 3), (3, 1)])  14.7 us
    reduce_scatter x1, waiting for transfers between devices, local(): lax.psum_scatter(partial, 'row', scatter_dimension=0, tiled=True)  12.4 us
    dot_general x3, matrix products, contract_tokens(): lax.dot_general(left, right, (((0,), (0,)), ((), ())), preferred_element_...  11.7 us
    ppermute x3, starting transfers between devices, swap_far(): return lax.ppermute(x, 'dp', [(0, 2), (2, 0), (1, 3), (3, 1)])  6.26 us
  transfers between devices with their start and end apart: 26, of which 12 were waited for; matrix products, arithmetic and copies ran while one was open for 20% of the time, Pallas kernels for 0%

profile of v2, /device:TPU:8, one launch (start us, length us, event | category | flops | bytes accessed | tf_op | source)
XLA Modules:
  0.0 255.5 jit_solution(10213469590103834058)
XLA Ops:
  7.2 1.6 fusion.9
  8.8 5.9 %collective-permute-start = (bf16[128,1792]{1,0:T(8,128)(2,1)S(1)}, bf16[128,1792]{1,0:T(8,128)(2,1)}, u32[]{:S(2)}, u32[]{:S(2)}) collective-permute-start(bf16[128,1792]{1,0:T(8,128)(2,1)S(1)} %fusion.9), channel_id=1, source_target_pairs={{0,56},{8,0},{16,8},{24,16},{32,24},{40,32},{48,40},{56,48},{1,57}... | collective-permute-start | bytes 1376264 | tf_op jit(solution)/shard_map/ppermute | solution.py:12
  14.7 2.0 broadcast_in_dim.6
  16.7 5.8 %all-to-all-start = ((bf16[8,128,512]{2,1,0:T(8,128)(2,1)}), bf16[8,128,512]{2,1,0:T(8,128)(2,1)S(1)}, u32[]{:S(2)}, u32[]{:S(2)}) async-start(bf16[8,128,512]{2,1,0:T(8,128)(2,1)} %broadcast_in_dim.6), calls=%async_computation | async-start | bytes 2097152 | tf_op jit(solution)/shard_map/all_to_all | solution.py:16
  22.5 1.9 collective-permute-done
  24.5 3.8 %collective-permute-start.1 = (bf16[128,1792]{1,0:T(8,128)(2,1)}, bf16[128,1792]{1,0:T(8,128)(2,1)S(1)}, u32[]{:S(2)}, u32[]{:S(2)}) collective-permute-start(bf16[128,1792]{1,0:T(8,128)(2,1)} %collective-permute-done), channel_id=1, source_target_pairs={{0,56},{8,0},{16,8},{24,16},{32,24},{40,32},{48,40},{56,48},{1,57}... | collective-permute-start | bytes 1376264 | tf_op jit(solution)/shard_map/ppermute | solution.py:12
  28.3 9.2 %collective-permute-done.1 = bf16[128,1792]{1,0:T(8,128)(2,1)S(1)} collective-permute-done((bf16[128,1792]{1,0:T(8,128)(2,1)}, bf16[128,1792]{1,0:T(8,128)(2,1)S(1)}, u32[]{:S(2)}, u32[]{:S(2)}) %collective-permute-start.1) | collective-permute-done | bytes 458784 | tf_op jit(solution)/shard_map/ppermute | solution.py:12
  37.5 0.8 copy-done.12
  38.3 2.6 %collective-permute-done.3 = bf16[128,1792]{1,0:T(8,128)(2,1)} collective-permute-done((bf16[128,1792]{1,0:T(8,128)(2,1)}, bf16[128,1792]{1,0:T(8,128)(2,1)}, u32[]{:S(2)}, u32[]{:S(2)}) %collective-permute-start.3) | collective-permute-done | bytes 458784 | tf_op jit(solution)/shard_map/ppermute | solution.py:12
  40.9 3.9 %convolution_convert_fusion = bf16[1024,1792]{1,0:T(8,128)(2,1)} fusion(bf16[1024,512]{1,0:T(8,128)(2,1)S(1)} %bitcast.69, bf16[512,1792]{1,0:T(8,128)(2,1)S(1)} %copy-done), kind=kOutput, calls=%fused_computation.2 | convolution fusion | flops 1880883200 | bytes 6553600 | tf_op jit(solution)/shard_map/dot_general | solution.py:81
  44.8 0.9 copy-done.15
  45.7 1.1 broadcast_in_dim.7
  46.8 5.8 %all-to-all-start.1 = ((bf16[8,128,512]{2,1,0:T(8,128)(2,1)}), bf16[8,128,512]{2,1,0:T(8,128)(2,1)S(1)}, u32[]{:S(2)}, u32[]{:S(2)}) async-start(bf16[8,128,512]{2,1,0:T(8,128)(2,1)} %broadcast_in_dim.7), calls=%async_computation.2 | async-start | bytes 2097152 | tf_op jit(solution)/shard_map/all_to_all | solution.py:16
  52.6 3.2 %collective-permute-start.4 = (bf16[128,1792]{1,0:T(8,128)(2,1)S(1)}, bf16[128,1792]{1,0:T(8,128)(2,1)}, u32[]{:S(2)}, u32[]{:S(2)}) collective-permute-start(bf16[128,1792]{1,0:T(8,128)(2,1)S(1)} %copy-done.13), channel_id=1, source_target_pairs={{0,56},{8,0},{16,8},{24,16},{32,24},{40,32},{48,40},{56,48},{1,57}... | collective-permute-start | bytes 1376264 | tf_op jit(solution)/shard_map/ppermute | solution.py:12
  55.9 19.8 %collective-permute-done.5 = bf16[128,1792]{1,0:T(8,128)(2,1)S(1)} collective-permute-done((bf16[128,1792]{1,0:T(8,128)(2,1)}, bf16[128,1792]{1,0:T(8,128)(2,1)S(1)}, u32[]{:S(2)}, u32[]{:S(2)}) %collective-permute-start.5) | collective-permute-done | bytes 458784 | tf_op jit(solution)/shard_map/ppermute | solution.py:12
  75.7 20.8 %collective-permute-done.6 = bf16[128,1792]{1,0:T(8,128)(2,1)} collective-permute-done((bf16[128,1792]{1,0:T(8,128)(2,1)S(1)}, bf16[128,1792]{1,0:T(8,128)(2,1)}, u32[]{:S(2)}, u32[]{:S(2)}) %collective-permute-start.6) | collective-permute-done | bytes 458784 | tf_op jit(solution)/shard_map/ppermute | solution.py:12
  96.6 12.4 %reduce-scatter.2.cloned.1.call-done = bf16[128,1792]{1,0:T(8,128)(2,1)} async-done(((bf16[1024,1792]{1,0:T(8,128)(2,1)}), bf16[128,1792]{1,0:T(8,128)(2,1)}) %reduce-scatter.2.cloned.1.call-update) | async-done | bytes 458768 | tf_op jit(solution)/shard_map/reduce_scatter | solution.py:84
  109.0 2.1 constant_dynamic-update-slice_fusion.7
  111.0 2.2 fusion.12
  113.2 0.8 constant_dynamic-update-slice_fusion.15
  114.1 0.8 collective-permute-start.8
  114.9 1.8 constant_dynamic-update-slice_fusion.14
  116.7 1.8 constant_dynamic-update-slice_fusion.13
  118.6 1.8 constant_dynamic-update-slice_fusion.12
  120.4 1.8 constant_dynamic-update-slice_fusion.11
  122.2 1.8 constant_dynamic-update-slice_fusion.10
  124.0 1.8 constant_dynamic-update-slice_fusion.9
  125.8 1.8 constant_dynamic-update-slice_fusion.8
  127.7 5.1 %fusion.4 = f32[512,1792]{1,0:T(8,128)S(1)} fusion(bf16[1024,1792]{1,0:T(8,128)(2,1)} %constant_dynamic-update-slice_fusion.8, s32[]{:T(128)S(6)} %select_n.41, bf16[1024,512]{1,0:T(8,128)(2,1)S(1)} %bitcast.70), kind=kOutput, calls=%fused_computation.24 | convolution fusion | flops 1881145344 | bytes 8388612 | tf_op jit(solution)/shard_map/dot_general | solution.py:56
  132.7 1.9 copy-done.6
  134.8 1.4 collective-permute-start.12
  136.2 2.0 collective-permute-start.9
  138.2 21.0 %collective-permute-done.12 = bf16[128,1792]{1,0:T(8,128)(2,1)S(1)} collective-permute-done((bf16[128,1792]{1,0:T(8,128)(2,1)S(1)}, bf16[128,1792]{1,0:T(8,128)(2,1)S(1)}, u32[]{:S(2)}, u32[]{:S(2)}) %collective-permute-start.12) | collective-permute-done | bytes 458784 | tf_op jit(solution)/shard_map/ppermute | solution.py:12
  159.1 1.8 constant_dynamic-update-slice_fusion.6
  161.0 3.2 %collective-permute-start.10 = (bf16[128,1792]{1,0:T(8,128)(2,1)}, bf16[128,1792]{1,0:T(8,128)(2,1)S(1)}, u32[]{:S(2)}, u32[]{:S(2)}) collective-permute-start(bf16[128,1792]{1,0:T(8,128)(2,1)} %collective-permute-done.9), channel_id=1, source_target_pairs={{0,56},{8,0},{16,8},{24,16},{32,24},{40,32},{48,40},{56,48},{1,57}... | collective-permute-start | bytes 1376264 | tf_op jit(solution)/shard_map/ppermute | solution.py:12
  164.2 2.0 bitcast_add_fusion
  166.2 0.9 fusion.24
  167.1 2.7 %collective-permute-start.20 = (bf16[128,1792]{1,0:T(8,128)(2,1)}, bf16[128,1792]{1,0:T(8,128)(2,1)}, u32[]{:S(2)}, u32[]{:S(2)}) collective-permute-start(bf16[128,1792]{1,0:T(8,128)(2,1)} %fusion.24), channel_id=1, source_target_pairs={{0,128},{128,0},{64,192},{192,64},{1,129},{129,1},{65,193},{193,65... | collective-permute-start | bytes 1376264 | tf_op jit(solution)/shard_map/ppermute | solution.py:35
  169.8 11.6 %collective-permute-done.13 = bf16[128,1792]{1,0:T(8,128)(2,1)S(1)} collective-permute-done((bf16[128,1792]{1,0:T(8,128)(2,1)S(1)}, bf16[128,1792]{1,0:T(8,128)(2,1)S(1)}, u32[]{:S(2)}, u32[]{:S(2)}) %collective-permute-start.13) | collective-permute-done | bytes 458784 | tf_op jit(solution)/shard_map/ppermute | solution.py:12
  181.4 3.2 %collective-permute-start.11 = (bf16[128,1792]{1,0:T(8,128)(2,1)S(1)}, bf16[128,1792]{1,0:T(8,128)(2,1)S(1)}, u32[]{:S(2)}, u32[]{:S(2)}) collective-permute-start(bf16[128,1792]{1,0:T(8,128)(2,1)S(1)} %collective-permute-done.10), channel_id=1, source_target_pairs={{0,56},{8,0},{16,8},{24,16},{32,24},{40,32},{48,40},{56,48},{1,57}... | collective-permute-start | bytes 1376264 | tf_op jit(solution)/shard_map/ppermute | solution.py:12
  184.6 1.0 constant_dynamic-update-slice_fusion.5
  185.7 8.3 %collective-permute-done.11 = bf16[128,1792]{1,0:T(8,128)(2,1)S(1)} collective-permute-done((bf16[128,1792]{1,0:T(8,128)(2,1)S(1)}, bf16[128,1792]{1,0:T(8,128)(2,1)S(1)}, u32[]{:S(2)}, u32[]{:S(2)}) %collective-permute-start.11) | collective-permute-done | bytes 458784 | tf_op jit(solution)/shard_map/ppermute | solution.py:12
  194.0 0.7 collective-permute-done.14
  194.8 2.3 fusion.7
  197.1 1.8 copy-done.7
  199.3 3.5 %fusion.33 = f32[1024,512]{1,0:T(8,128)} fusion(bf16[1024,1792]{1,0:T(8,128)(2,1)S(1)} %constant_dynamic-update-slice_fusion, bf16[1792,512]{1,0:T(8,128)(2,1)S(1)} %copy-done.18), kind=kOutput, calls=%fused_computation.75 | convolution fusion | flops 1879048192 | bytes 7602176 | tf_op jit(solution)/shard_map/dot_general | solution.py:107
  202.8 4.3 %fusion.32 = f32[1792,512]{1,0:T(8,128)S(1)} fusion(bf16[1024,1792]{1,0:T(8,128)(2,1)} %all-gather.2.cloned.1.call-done, bf16[1024,512]{1,0:T(8,128)(2,1)S(1)} %bitcast.68), kind=kOutput, calls=%fused_computation.74 | convolution fusion | flops 1879048192 | bytes 8388608 | tf_op jit(solution)/shard_map/dot_general | solution.py:56
  207.3 0.6 collective-permute-start.7
  207.8 1.9 bitcast_add_fusion.1
  209.7 0.9 fusion.23
  210.7 2.1 fusion.2
  212.8 1.1 copy.22
  214.2 1.3 copy-done.2
  215.5 0.8 fusion.22
  216.3 4.8 %all-to-all-start.2 = ((bf16[4,2,128,512]{3,2,1,0:T(8,128)(2,1)}), bf16[4,2,128,512]{3,2,1,0:T(8,128)(2,1)S(1)}, u32[]{:S(2)}, u32[]{:S(2)}) async-start(bf16[4,2,128,512]{3,2,1,0:T(8,128)(2,1)} %bitcast.60), calls=%async_computation.3 | async-start | bytes 2097152 | tf_op jit(solution)/shard_map/all_to_all | solution.py:16
  221.1 3.0 %collective-permute-start.18 = (bf16[448,512]{1,0:T(8,128)(2,1)}, bf16[448,512]{1,0:T(8,128)(2,1)S(1)}, u32[]{:S(2)}, u32[]{:S(2)}) collective-permute-start(bf16[448,512]{1,0:T(8,128)(2,1)} %fusion.23), channel_id=1, source_target_pairs={{0,128},{128,0},{64,192},{192,64},{1,129},{129,1},{65,193},{193,65... | collective-permute-start | bytes 1376264 | tf_op jit(solution)/shard_map/ppermute | solution.py:35
  224.1 2.5 bitcast_add_fusion.3
  226.6 0.6 collective-permute-start.17
  227.1 9.2 %collective-permute-done.18 = bf16[448,512]{1,0:T(8,128)(2,1)S(1)} collective-permute-done((bf16[448,512]{1,0:T(8,128)(2,1)}, bf16[448,512]{1,0:T(8,128)(2,1)S(1)}, u32[]{:S(2)}, u32[]{:S(2)}) %collective-permute-start.18) | collective-permute-done | bytes 458784 | tf_op jit(solution)/shard_map/ppermute | solution.py:35
  236.3 2.2 bitcast_add_fusion.4
  238.7 1.6 collective-permute-start.16
  240.3 5.5 %collective-permute-done.17 = bf16[448,512]{1,0:T(8,128)(2,1)S(1)} collective-permute-done((bf16[448,512]{1,0:T(8,128)(2,1)}, bf16[448,512]{1,0:T(8,128)(2,1)S(1)}, u32[]{:S(2)}, u32[]{:S(2)}) %collective-permute-start.17) | collective-permute-done | bytes 458784 | tf_op jit(solution)/shard_map/ppermute | solution.py:35
  245.8 2.2 bitcast_add_fusion.5
  248.0 0.7 fusion.25
  (74 shorter events, 1.5 us)
Async XLA Ops:
  7.2 33.7 %copy-start = (bf16[512,1792]{1,0:T(8,128)(2,1)S(1)}, bf16[512,1792]{1,0:T(8,128)(2,1)}, u32[]{:S(2)}) copy-start(bf16[512,1792]{1,0:T(8,128)(2,1)} %param.13) | copy-start | bytes 5505028
  8.8 15.7 %collective-permute-start = (bf16[128,1792]{1,0:T(8,128)(2,1)S(1)}, bf16[128,1792]{1,0:T(8,128)(2,1)}, u32[]{:S(2)}, u32[]{:S(2)}) collective-permute-start(bf16[128,1792]{1,0:T(8,128)(2,1)S(1)} %fusion.9), channel_id=1, source_target_pairs={{0,56},{8,0},{16,8},{24,16},{32,24},{40,32},{48,40},{56,48},{1,57}... | collective-permute-start | bytes 1376264 | tf_op jit(solution)/shard_map/ppermute | solution.py:12
  14.7 13.6 %collective-permute-start.2 = (bf16[128,1792]{1,0:T(8,128)(2,1)S(1)}, bf16[128,1792]{1,0:T(8,128)(2,1)}, u32[]{:S(2)}, u32[]{:S(2)}) collective-permute-start(bf16[128,1792]{1,0:T(8,128)(2,1)S(1)} %fusion.9), channel_id=1, source_target_pairs={{0,8},{8,16},{16,24},{24,32},{32,40},{40,48},{48,56},{56,0},{1,9},... | collective-permute-start | bytes 1376264 | tf_op jit(solution)/shard_map/ppermute | solution.py:12
  16.7 24.2 %all-to-all-start = ((bf16[8,128,512]{2,1,0:T(8,128)(2,1)}), bf16[8,128,512]{2,1,0:T(8,128)(2,1)S(1)}, u32[]{:S(2)}, u32[]{:S(2)}) async-start(bf16[8,128,512]{2,1,0:T(8,128)(2,1)} %broadcast_in_dim.6), calls=%async_computation | async-start | bytes 2097152 | tf_op jit(solution)/shard_map/all_to_all | solution.py:16
  22.5 86.4 %reduce-scatter.2.cloned.1.call-start = ((), (), s32[]{:S(2)}) async-start(), calls=%async_computation.4 | async-start | bytes 4128768 | tf_op jit(solution)/shard_map/reduce_scatter | solution.py:84
  24.5 13.0 %collective-permute-start.1 = (bf16[128,1792]{1,0:T(8,128)(2,1)}, bf16[128,1792]{1,0:T(8,128)(2,1)S(1)}, u32[]{:S(2)}, u32[]{:S(2)}) collective-permute-start(bf16[128,1792]{1,0:T(8,128)(2,1)} %collective-permute-done), channel_id=1, source_target_pairs={{0,56},{8,0},{16,8},{24,16},{32,24},{40,32},{48,40},{56,48},{1,57}... | collective-permute-start | bytes 1376264 | tf_op jit(solution)/shard_map/ppermute | solution.py:12
  28.3 12.6 %collective-permute-start.3 = (bf16[128,1792]{1,0:T(8,128)(2,1)}, bf16[128,1792]{1,0:T(8,128)(2,1)}, u32[]{:S(2)}, u32[]{:S(2)}) collective-permute-start(bf16[128,1792]{1,0:T(8,128)(2,1)} %collective-permute-done.2), channel_id=1, source_target_pairs={{0,8},{8,16},{16,24},{24,32},{32,40},{40,48},{48,56},{56,0},{1,9},... | collective-permute-start | bytes 1376264 | tf_op jit(solution)/shard_map/ppermute | solution.py:12
  37.5 0.8 copy-start.12
  40.9 3.9 %copy-start.10 = (bf16[8,128,512]{2,1,0:T(8,128)(2,1)}, bf16[8,128,512]{2,1,0:T(8,128)(2,1)S(1)}, u32[]{:S(2)}) copy-start(bf16[8,128,512]{2,1,0:T(8,128)(2,1)S(1)} %all-to-all-done) | copy-start | bytes 3145732
  44.8 0.9 copy-start.15
  44.8 7.8 %copy-start.13 = (bf16[128,1792]{1,0:T(8,128)(2,1)S(1)}, bf16[128,1792]{1,0:T(8,128)(2,1)}, u32[]{:S(2)}) copy-start(bf16[128,1792]{1,0:T(8,128)(2,1)} %copy-done.12) | copy-start | bytes 1376260
  44.8 64.2 %copy-start.5 = (bf16[128,1792]{1,0:T(8,128)(2,1)S(1)}, bf16[128,1792]{1,0:T(8,128)(2,1)}, u32[]{:S(2)}) copy-start(bf16[128,1792]{1,0:T(8,128)(2,1)} %param.9) | copy-start | bytes 1376260
  44.8 66.2 %copy-start.9 = (bf16[128,1792]{1,0:T(8,128)(2,1)S(1)}, bf16[128,1792]{1,0:T(8,128)(2,1)}, u32[]{:S(2)}) copy-start(bf16[128,1792]{1,0:T(8,128)(2,1)} %param.10) | copy-start | bytes 1376260
  46.8 28.9 %all-to-all-start.1 = ((bf16[8,128,512]{2,1,0:T(8,128)(2,1)}), bf16[8,128,512]{2,1,0:T(8,128)(2,1)S(1)}, u32[]{:S(2)}, u32[]{:S(2)}) async-start(bf16[8,128,512]{2,1,0:T(8,128)(2,1)} %broadcast_in_dim.7), calls=%async_computation.2 | async-start | bytes 2097152 | tf_op jit(solution)/shard_map/all_to_all | solution.py:16
  52.6 150.2 %all-gather.2.cloned.1.call-start = ((), (), s32[]{:S(2)}) async-start(), calls=%async_computation.5 | async-start | bytes 4128768 | tf_op jit(solution)/shard_map/all_gather | solution.py:91
  52.6 23.1 %collective-permute-start.5 = (bf16[128,1792]{1,0:T(8,128)(2,1)}, bf16[128,1792]{1,0:T(8,128)(2,1)S(1)}, u32[]{:S(2)}, u32[]{:S(2)}) collective-permute-start(bf16[128,1792]{1,0:T(8,128)(2,1)} %collective-permute-done.3), channel_id=1, source_target_pairs={{0,8},{8,16},{16,24},{24,32},{32,40},{40,48},{48,56},{56,0},{1,9},... | collective-permute-start | bytes 1376264 | tf_op jit(solution)/shard_map/ppermute | solution.py:12
  52.6 23.1 %collective-permute-start.4 = (bf16[128,1792]{1,0:T(8,128)(2,1)S(1)}, bf16[128,1792]{1,0:T(8,128)(2,1)}, u32[]{:S(2)}, u32[]{:S(2)}) collective-permute-start(bf16[128,1792]{1,0:T(8,128)(2,1)S(1)} %copy-done.13), channel_id=1, source_target_pairs={{0,56},{8,0},{16,8},{24,16},{32,24},{40,32},{48,40},{56,48},{1,57}... | collective-permute-start | bytes 1376264 | tf_op jit(solution)/shard_map/ppermute | solution.py:12
  75.7 33.3 %copy-start.14 = (bf16[128,1792]{1,0:T(8,128)(2,1)}, bf16[128,1792]{1,0:T(8,128)(2,1)S(1)}, u32[]{:S(2)}) copy-start(bf16[128,1792]{1,0:T(8,128)(2,1)S(1)} %collective-permute-done.5) | copy-start | bytes 1376260
  75.7 20.9 %collective-permute-start.6 = (bf16[128,1792]{1,0:T(8,128)(2,1)S(1)}, bf16[128,1792]{1,0:T(8,128)(2,1)}, u32[]{:S(2)}, u32[]{:S(2)}) collective-permute-start(bf16[128,1792]{1,0:T(8,128)(2,1)S(1)} %collective-permute-done.5), channel_id=1, source_target_pairs={{0,8},{8,16},{16,24},{24,32},{32,40},{40,48},{48,56},{56,0},{1,9},... | collective-permute-start | bytes 1376264 | tf_op jit(solution)/shard_map/ppermute | solution.py:12
  114.1 13.6 %copy-start.11 = (bf16[8,128,512]{2,1,0:T(8,128)(2,1)S(1)}, bf16[8,128,512]{2,1,0:T(8,128)(2,1)}, u32[]{:S(2)}) copy-start(bf16[8,128,512]{2,1,0:T(8,128)(2,1)} %copy-done.10) | copy-start | bytes 3145732
  114.1 22.1 %collective-permute-start.8 = (bf16[128,1792]{1,0:T(8,128)(2,1)S(1)}, bf16[128,1792]{1,0:T(8,128)(2,1)}, u32[]{:S(2)}, u32[]{:S(2)}) collective-permute-start(bf16[128,1792]{1,0:T(8,128)(2,1)S(1)} %get-tuple-element.45), channel_id=1, source_target_pairs={{0,56},{8,0},{16,8},{24,16},{32,24},{40,32},{48,40},{56,48},{1,57}... | collective-permute-start | bytes 1376264 | tf_op jit(solution)/shard_map/ppermute | solution.py:12
  132.7 1.9 copy-start.6
  134.7 29.5 %collective-permute-start.19 = (bf16[2,128,1792]{2,1,0:T(8,128)(2,1)S(1)}, bf16[2,128,1792]{2,1,0:T(8,128)(2,1)}, u32[]{:S(2)}, u32[]{:S(2)}) collective-permute-start(bf16[2,128,1792]{2,1,0:T(8,128)(2,1)S(1)} %fusion.21), channel_id=1, source_target_pairs={{0,64},{64,0},{128,192},{192,128},{1,65},{65,1},{129,193},{193,129... | collective-permute-start | bytes 2752520 | tf_op jit(solution)/shard_map/ppermute | solution.py:28
  134.8 24.3 %collective-permute-start.12 = (bf16[128,1792]{1,0:T(8,128)(2,1)S(1)}, bf16[128,1792]{1,0:T(8,128)(2,1)S(1)}, u32[]{:S(2)}, u32[]{:S(2)}) collective-permute-start(bf16[128,1792]{1,0:T(8,128)(2,1)S(1)} %get-tuple-element.45), channel_id=1, source_target_pairs={{0,8},{8,16},{16,24},{24,32},{32,40},{40,48},{48,56},{56,0},{1,9},... | collective-permute-start | bytes 1376264 | tf_op jit(solution)/shard_map/ppermute | solution.py:12
  136.2 24.8 %collective-permute-start.9 = (bf16[128,1792]{1,0:T(8,128)(2,1)}, bf16[128,1792]{1,0:T(8,128)(2,1)}, u32[]{:S(2)}, u32[]{:S(2)}) collective-permute-start(bf16[128,1792]{1,0:T(8,128)(2,1)} %collective-permute-done.8), channel_id=1, source_target_pairs={{0,56},{8,0},{16,8},{24,16},{32,24},{40,32},{48,40},{56,48},{1,57}... | collective-permute-start | bytes 1376264 | tf_op jit(solution)/shard_map/ppermute | solution.py:12
  159.1 22.2 %collective-permute-start.13 = (bf16[128,1792]{1,0:T(8,128)(2,1)S(1)}, bf16[128,1792]{1,0:T(8,128)(2,1)S(1)}, u32[]{:S(2)}, u32[]{:S(2)}) collective-permute-start(bf16[128,1792]{1,0:T(8,128)(2,1)S(1)} %collective-permute-done.12), channel_id=1, source_target_pairs={{0,8},{8,16},{16,24},{24,32},{32,40},{40,48},{48,56},{56,0},{1,9},... | collective-permute-start | bytes 1376264 | tf_op jit(solution)/shard_map/ppermute | solution.py:12
  161.0 23.6 %copy-start.16 = (bf16[1024,1792]{1,0:T(8,128)(2,1)S(1)}, bf16[1024,1792]{1,0:T(8,128)(2,1)}, u32[]{:S(2)}) copy-start(bf16[1024,1792]{1,0:T(8,128)(2,1)} %constant_dynamic-update-slice_fusion.6) | copy-start | bytes 11010052
  161.0 20.4 %collective-permute-start.10 = (bf16[128,1792]{1,0:T(8,128)(2,1)}, bf16[128,1792]{1,0:T(8,128)(2,1)S(1)}, u32[]{:S(2)}, u32[]{:S(2)}) collective-permute-start(bf16[128,1792]{1,0:T(8,128)(2,1)} %collective-permute-done.9), channel_id=1, source_target_pairs={{0,56},{8,0},{16,8},{24,16},{32,24},{40,32},{48,40},{56,48},{1,57}... | collective-permute-start | bytes 1376264 | tf_op jit(solution)/shard_map/ppermute | solution.py:12
  166.2 30.9 %copy-start.4 = (f32[2,128,1792]{2,1,0:T(8,128)}, f32[2,128,1792]{2,1,0:T(8,128)S(1)}, u32[]{:S(2)}) copy-start(f32[2,128,1792]{2,1,0:T(8,128)S(1)} %bitcast_add_fusion) | copy-start | bytes 5505028
  167.1 57.0 %collective-permute-start.20 = (bf16[128,1792]{1,0:T(8,128)(2,1)}, bf16[128,1792]{1,0:T(8,128)(2,1)}, u32[]{:S(2)}, u32[]{:S(2)}) collective-permute-start(bf16[128,1792]{1,0:T(8,128)(2,1)} %fusion.24), channel_id=1, source_target_pairs={{0,128},{128,0},{64,192},{192,64},{1,129},{129,1},{65,193},{193,65... | collective-permute-start | bytes 1376264 | tf_op jit(solution)/shard_map/ppermute | solution.py:35
  181.3 13.3 %collective-permute-start.14 = (bf16[128,1792]{1,0:T(8,128)(2,1)S(1)}, bf16[128,1792]{1,0:T(8,128)(2,1)S(1)}, u32[]{:S(2)}, u32[]{:S(2)}) collective-permute-start(bf16[128,1792]{1,0:T(8,128)(2,1)S(1)} %collective-permute-done.13), channel_id=1, source_target_pairs={{0,8},{8,16},{16,24},{24,32},{32,40},{40,48},{48,56},{56,0},{1,9},... | collective-permute-start | bytes 1376264 | tf_op jit(solution)/shard_map/ppermute | solution.py:12
  181.4 12.6 %collective-permute-start.11 = (bf16[128,1792]{1,0:T(8,128)(2,1)S(1)}, bf16[128,1792]{1,0:T(8,128)(2,1)S(1)}, u32[]{:S(2)}, u32[]{:S(2)}) collective-permute-start(bf16[128,1792]{1,0:T(8,128)(2,1)S(1)} %collective-permute-done.10), channel_id=1, source_target_pairs={{0,56},{8,0},{16,8},{24,16},{32,24},{40,32},{48,40},{56,48},{1,57}... | collective-permute-start | bytes 1376264 | tf_op jit(solution)/shard_map/ppermute | solution.py:12
  194.8 4.5 %copy-start.18 = (bf16[1792,512]{1,0:T(8,128)(2,1)S(1)}, bf16[1792,512]{1,0:T(8,128)(2,1)}, u32[]{:S(2)}) copy-start(bf16[1792,512]{1,0:T(8,128)(2,1)} %param.12) | copy-start | bytes 5505028
  197.1 1.8 copy-start.7
  199.0 8.8 %collective-permute-start.15 = (bf16[2,448,512]{2,1,0:T(8,128)(2,1)S(1)}, bf16[2,448,512]{2,1,0:T(8,128)(2,1)}, u32[]{:S(2)}, u32[]{:S(2)}) collective-permute-start(bf16[2,448,512]{2,1,0:T(8,128)(2,1)S(1)} %fusion.20), channel_id=1, source_target_pairs={{0,64},{64,0},{128,192},{192,128},{1,65},{65,1},{129,193},{193,129... | collective-permute-start | bytes 2752520 | tf_op jit(solution)/shard_map/ppermute | solution.py:28
  202.8 5.1 %copy-start.8 = (f32[1792,512]{1,0:T(8,128)S(1)}, f32[1792,512]{1,0:T(8,128)}, u32[]{:S(2)}) copy-start(f32[1792,512]{1,0:T(8,128)} %copy-done.7) | copy-start | bytes 11010052
  202.8 7.9 %copy-start.20 = (f32[1024,512]{1,0:T(8,128)S(1)}, f32[1024,512]{1,0:T(8,128)}, u32[]{:S(2)}) copy-start(f32[1024,512]{1,0:T(8,128)} %fusion.33) | copy-start | bytes 6291460
  207.1 3.6 %copy-start.17 = (bf16[1024,1792]{1,0:T(8,128)(2,1)S(1)}, bf16[1024,1792]{1,0:T(8,128)(2,1)}, u32[]{:S(2)}) copy-start(bf16[1024,1792]{1,0:T(8,128)(2,1)} %all-gather.2.cloned.1.call-done) | copy-start | bytes 11010052
  207.1 3.5 %copy-start.19 = (bf16[1792,512]{1,0:T(8,128)(2,1)S(1)}, bf16[1792,512]{1,0:T(8,128)(2,1)}, u32[]{:S(2)}) copy-start(bf16[1792,512]{1,0:T(8,128)(2,1)} %param.11) | copy-start | bytes 5505028
  207.3 6.6 %collective-permute-start.7 = (bf16[2,448,512]{2,1,0:T(8,128)(2,1)S(1)}, bf16[2,448,512]{2,1,0:T(8,128)(2,1)S(1)}, u32[]{:S(2)}, u32[]{:S(2)}) collective-permute-start(bf16[2,448,512]{2,1,0:T(8,128)(2,1)S(1)} %fusion.19), channel_id=1, source_target_pairs={{0,64},{64,0},{128,192},{192,128},{1,65},{65,1},{129,193},{193,129... | collective-permute-start | bytes 2752520 | tf_op jit(solution)/shard_map/ppermute | solution.py:28
  209.7 3.1 %copy-start.3 = (f32[2,448,512]{2,1,0:T(8,128)}, f32[2,448,512]{2,1,0:T(8,128)S(1)}, u32[]{:S(2)}) copy-start(f32[2,448,512]{2,1,0:T(8,128)S(1)} %bitcast_add_fusion.1) | copy-start | bytes 5505028
  214.2 1.3 copy-start.2
  216.3 22.2 %all-to-all-start.2 = ((bf16[4,2,128,512]{3,2,1,0:T(8,128)(2,1)}), bf16[4,2,128,512]{3,2,1,0:T(8,128)(2,1)S(1)}, u32[]{:S(2)}, u32[]{:S(2)}) async-start(bf16[4,2,128,512]{3,2,1,0:T(8,128)(2,1)} %bitcast.60), calls=%async_computation.3 | async-start | bytes 2097152 | tf_op jit(solution)/shard_map/all_to_all | solution.py:16
  221.1 15.2 %collective-permute-start.18 = (bf16[448,512]{1,0:T(8,128)(2,1)}, bf16[448,512]{1,0:T(8,128)(2,1)S(1)}, u32[]{:S(2)}, u32[]{:S(2)}) collective-permute-start(bf16[448,512]{1,0:T(8,128)(2,1)} %fusion.23), channel_id=1, source_target_pairs={{0,128},{128,0},{64,192},{192,64},{1,129},{129,1},{65,193},{193,65... | collective-permute-start | bytes 1376264 | tf_op jit(solution)/shard_map/ppermute | solution.py:35
  224.1 24.6 %copy-start.1 = (bf16[512,1792]{1,0:T(8,128)(2,1)S(1)}, bf16[512,1792]{1,0:T(8,128)(2,1)}, u32[]{:S(2)}) copy-start(bf16[512,1792]{1,0:T(8,128)(2,1)} %param.13) | copy-start | bytes 5505028
  226.6 19.2 %collective-permute-start.17 = (bf16[448,512]{1,0:T(8,128)(2,1)}, bf16[448,512]{1,0:T(8,128)(2,1)S(1)}, u32[]{:S(2)}, u32[]{:S(2)}) collective-permute-start(bf16[448,512]{1,0:T(8,128)(2,1)} %fusion.22), channel_id=1, source_target_pairs={{0,128},{128,0},{64,192},{192,64},{1,129},{129,1},{65,193},{193,65... | collective-permute-start | bytes 1376264 | tf_op jit(solution)/shard_map/ppermute | solution.py:35
  238.7 9.3 %collective-permute-start.16 = (bf16[128,512]{1,0:T(8,128)(2,1)S(1)}, bf16[128,512]{1,0:T(8,128)(2,1)S(1)}, u32[]{:S(2)}, u32[]{:S(2)}) collective-permute-start(bf16[128,512]{1,0:T(8,128)(2,1)S(1)} %fusion.26), channel_id=1, source_target_pairs={{0,4},{1,5},{2,6},{3,7},{4,0},{5,1},{6,2},{7,3},{8,12},{9,13},{10,... | collective-permute-start | bytes 393224 | tf_op jit(solution)/shard_map/ppermute | solution.py:39
Sparse Core Ops, SparseCore 0:
  45.0 63.9 reduce-scatter.1
  115.0 65.8 all-gather.1

commit v3 on v1

v3 whole, which is shorter than its diff:
```python
import jax
import jax.numpy as jnp
from jax import lax
from jax.sharding import PartitionSpec as P

F32 = jnp.float32
BF16 = jnp.bfloat16
ROWS = 8


def shift_row(x, step):
    return lax.ppermute(x, "row", [(i, (i + step) % ROWS) for i in range(ROWS)])


def exchange(x, axis, groups=None):
    return lax.all_to_all(x, axis, 0, 0, axis_index_groups=groups, tiled=True)


def spread_col(x):
    return jnp.broadcast_to(x, (8,) + x.shape)


def pick(x, at, axis):
    return lax.dynamic_index_in_dim(x, at, axis, keepdims=False)


def halve_core(x, core):
    other = lax.ppermute(
        pick(x, 1 - core, 1).astype(BF16), "dp", [(0, 1), (1, 0), (2, 3), (3, 2)]
    )
    return pick(x, core, 1) + other.astype(F32)


def gather_row(x, sign):
    blocks = [None] * ROWS
    blocks[0] = up = down = x
    for step in range(1, 5):
        if step < 4 or sign > 0:
            up = shift_row(up, 1)
            blocks[ROWS - step] = up
        if step < 4 or sign < 0:
            down = shift_row(down, -1)
            blocks[step] = down
    return blocks


def reduce_row(part, later, sooner):
    def add(o, b):
        return (part(o).astype(F32) + b.astype(F32)).astype(BF16)

    up, down = shift_row(part(4), 1), shift_row(part(5), -1)
    up, down, later = lax.optimization_barrier((up, down, later))
    up, down = shift_row(add(3, up), 1), shift_row(add(6, down), -1)
    up, down, sooner = lax.optimization_barrier((up, down, sooner))
    up, down = shift_row(add(2, up), 1), shift_row(add(7, down), -1)
    up = shift_row(add(1, up), 1)
    return part(0).astype(F32) + up.astype(F32) + down.astype(F32), later, sooner


def contract_tokens(left, right):
    return lax.dot_general(left, right, (((0,), (0,)), ((), ())), preferred_element_type=F32)


def local(tokens, cotangent, gate_pre, up_pre, w_gate, w_up, w_down):
    row = lax.axis_index("row")
    dp = lax.axis_index("dp")
    far, core = dp >> 1, dp & 1
    block, hidden_width = gate_pre.shape
    features = w_gate.shape[1]
    width = hidden_width // 2

    def turned(x, by):
        twice = jnp.concatenate([x, x], axis=0)
        return lax.dynamic_slice_in_dim(twice, by * block, ROWS * block, 0)

    def hidden_gradients(hidden_grad, low):
        cols = slice(low, low + width)
        gate_value = gate_pre[:, cols].astype(F32)
        up_value = up_pre[:, cols].astype(F32)
        sigmoid_gate = jax.nn.sigmoid(gate_value)
        gate_grad = hidden_grad * up_value * sigmoid_gate * (1.0 + gate_value * (1.0 - sigmoid_gate))
        up_grad = hidden_grad * gate_value * sigmoid_gate
        return jnp.concatenate([gate_grad.astype(BF16), up_grad.astype(BF16)], axis=1)

    def stacked_weights(low):
        return jnp.concatenate([w_gate[low : low + width], w_up[low : low + width]], axis=0)

    gate_value = gate_pre.astype(F32)
    hidden = (gate_value * jax.nn.sigmoid(gate_value) * up_pre.astype(F32)).astype(BF16)
    hidden_all = lax.all_gather(hidden, "row", axis=0, tiled=True)
    cot = exchange(spread_col(cotangent), "col").reshape(-1, features)

    first = jnp.dot(cot, w_down[:, :width], preferred_element_type=F32).astype(BF16)
    second = jnp.dot(cot, w_down[:, width:], preferred_element_type=F32).astype(BF16)
    parts = first.reshape(ROWS, block, width)
    first_sum, second, hidden_all = reduce_row(
        lambda o: pick(parts, (row + o) & 7, 0), second, hidden_all
    )
    second_sum = lax.psum_scatter(second, "row", scatter_dimension=0, tiled=True)
    first_sum, tokens = lax.optimization_barrier((first_sum, tokens))
    tok = exchange(spread_col(tokens), "col").reshape(-1, features)
    first_blocks = gather_row(hidden_gradients(first_sum, 0), -1)
    second_sum, first_blocks[1], first_blocks[7] = lax.optimization_barrier(
        (second_sum, first_blocks[1], first_blocks[7])
    )
    second_all = lax.all_gather(
        hidden_gradients(second_sum.astype(F32), width), "row", axis=0, tiled=True
    )

    down = contract_tokens(cot, hidden_all)
    down = halve_core(down.reshape(2, 2, block, hidden_width), core)
    away = lax.ppermute(
        pick(down, 1 - far, 0).astype(BF16), "dp", [(0, 2), (2, 0), (1, 3), (3, 1)]
    )
    grad_down = pick(down, far, 0) + away.astype(F32)
    grad_down, first_blocks[4] = lax.optimization_barrier((grad_down, first_blocks[4]))

    first_all = jnp.concatenate(first_blocks, axis=0)
    grads = contract_tokens(first_all, turned(tok, row)).reshape(2, 2, -1, features)
    grads = halve_core(grads, core)
    first_grads = grads + lax.ppermute(grads.astype(BF16), "dp", [(2, 0), (3, 1)]).astype(F32)
    first_token_grad = jnp.dot(first_all, stacked_weights(0), preferred_element_type=F32)
    first_token_grad = turned(first_token_grad, (ROWS - row) & 7)
    second_all, first_grads, first_token_grad = lax.optimization_barrier(
        (second_all, first_grads, first_token_grad)
    )

    grads = lax.optimization_barrier(contract_tokens(second_all, tok))
    grads = halve_core(grads.reshape(2, 2, -1, features), core)
    away = grads.astype(BF16)
    token_grad = jnp.dot(second_all, stacked_weights(width), preferred_element_type=F32)
    token_grad = (token_grad + first_token_grad).astype(BF16)
    second_grads = grads + lax.ppermute(away, "dp", [(0, 2), (1, 3)]).astype(F32)
    token_grad, away = lax.optimization_barrier((token_grad, away))
    token_grad = exchange(token_grad.reshape(8, block, features), "col")
    d_tokens = jnp.sum(token_grad.astype(F32), axis=0).astype(BF16)
    grads = jnp.where(far == 0, first_grads, second_grads)
    return (d_tokens, grads[0], grads[1], grad_down)


def solution(mesh):
    placed = (
        P(("dp", "col"), "row"),
        P(("dp", "col"), "row"),
        P(("dp", "row"), "col"),
        P(("dp", "row"), "col"),
        P("col", "row"),
        P("col", "row"),
        P("row", "col"),
    )
    return jax.shard_map(
        local,
        mesh=mesh,
        in_specs=placed,
        out_specs=(
            P(("dp", "col"), "row"),
            P(("col", "dp"), "row"),
            P(("col", "dp"), "row"),
            P(("row", "dp"), "col"),
        ),
        check_vma=False,
    )
```

time: 296 us -> 285 us (0.963)
  waiting for transfers between devices: 127 us -> 158 us
  blocking collectives: 14.4 us -> 0 us
  starting transfers between devices: 58.6 us -> 46.8 us
  local copies, waits for them, and re-layouts: 30.1 us -> 18.6 us
  matrix products: 30.3 us -> 26.2 us
    ppermute x0 -> x6, waiting for transfers between devices: none -> 32.7 us  [the longest x1 16.2 us: local(): lax.ppermute(grads.astype(BF16), 'dp', [(2, 0), (3, 1)]).astype(F32)]
    ppermute x14, waiting for transfers between devices: 98.9 us -> 81.6 us  [shift_row(): return lax.ppermute(x, 'row', [(i, (i + step) % ROWS) for i in range(ROWS)])]
    all_to_all x7 -> x3, starting transfers between devices: 34.5 us -> 17.3 us  [exchange(): return lax.all_to_all(x, axis, 0, 0, axis_index_groups=groups, tiled=True)]
    all_to_all x2 -> x0, blocking collectives: 14.4 us -> none  [exchange(): return lax.all_to_all(x, axis, 0, 0, axis_index_groups=groups, tiled=True)]
    reduce_scatter x1, waiting for transfers between devices: 7.33 us -> 14.9 us  [local(): lax.psum_scatter(second, 'row', scatter_dimension=0, tiled=True)]
    ppermute x0 -> x6, starting transfers between devices: none -> 6.74 us  [the longest x1 2.77 us: local(): lax.ppermute(pick(down, 1 - far, 0).astype(BF16), 'dp', [(0, 2), (2, 0),...]
    all_gather x1 -> x2, waiting for transfers between devices: 0.01 us -> 6.56 us  [the longest x1 6.54 us: local(): hidden_all = lax.all_gather(hidden, 'row', axis=0, tiled=True)]
    unnamed x51 -> x42, local copies, waits for them, and re-layouts: 15.3 us -> 8.77 us
  transfers between devices with their start and end apart: 23 -> 26, of which waited for: 15 -> 16; matrix products, arithmetic and copies ran while one was open for 22% -> 18% of each run, Pallas kernels for 0% -> 0%
where the time goes in v3:
time: 285 us; the launch traced here: 284 us
  waiting for transfers between devices  158 us (55%)
  starting transfers between devices  46.8 us (16%)
  matrix products  26.2 us (9%)
  other arithmetic  20.5 us (7%)
  local copies, waits for them, and re-layouts  18.6 us (7%)
  between operations  14 us (5%)
    ppermute x14, waiting for transfers between devices, shift_row(): return lax.ppermute(x, 'row', [(i, (i + step) % ROWS) for i in range(ROWS)])  81.6 us
    ppermute x14, starting transfers between devices, shift_row(): return lax.ppermute(x, 'row', [(i, (i + step) % ROWS) for i in range(ROWS)])  22.7 us
    all_to_all x3, waiting for transfers between devices, exchange(): return lax.all_to_all(x, axis, 0, 0, axis_index_groups=groups, tiled=True)  22 us
    all_to_all x3, starting transfers between devices, exchange(): return lax.all_to_all(x, axis, 0, 0, axis_index_groups=groups, tiled=True)  17.3 us
    ppermute x1, waiting for transfers between devices, local(): lax.ppermute(grads.astype(BF16), 'dp', [(2, 0), (3, 1)]).astype(F32)  16.2 us
    reduce_scatter x1, waiting for transfers between devices, local(): lax.psum_scatter(second, 'row', scatter_dimension=0, tiled=True)  14.9 us
    dot_general x3, matrix products, contract_tokens(): lax.dot_general(left, right, (((0,), (0,)), ((), ())), preferred_element_...  13.7 us
    ppermute x1, waiting for transfers between devices, local(): lax.ppermute(away, 'dp', [(0, 2), (1, 3)]).astype(F32)  11.3 us
  transfers between devices with their start and end apart: 26, of which 16 were waited for; matrix products, arithmetic and copies ran while one was open for 18% of the time, Pallas kernels for 0%

profile of v3, /device:TPU:8, one launch (start us, length us, event | category | flops | bytes accessed | tf_op | source)
XLA Modules:
  0.0 284.0 jit_solution(4535750874140307706)
XLA Ops:
  7.2 2.2 fusion.23
  9.4 2.0 broadcast_in_dim.6
  11.4 5.8 %all-to-all-start = ((bf16[8,128,512]{2,1,0:T(8,128)(2,1)}), bf16[8,128,512]{2,1,0:T(8,128)(2,1)S(1)}, u32[]{:S(2)}, u32[]{:S(2)}) async-start(bf16[8,128,512]{2,1,0:T(8,128)(2,1)} %broadcast_in_dim.6), calls=%async_computation | async-start | bytes 2097152 | tf_op jit(solution)/shard_map/all_to_all | solution.py:16
  17.3 13.6 %all-to-all-done = bf16[8,128,512]{2,1,0:T(8,128)(2,1)S(1)} async-done(((bf16[8,128,512]{2,1,0:T(8,128)(2,1)}), bf16[8,128,512]{2,1,0:T(8,128)(2,1)S(1)}, u32[]{:S(2)}, u32[]{:S(2)}) %all-to-all-start) | async-done | bytes 1048608 | tf_op jit(solution)/shard_map/all_to_all | solution.py:16
  30.9 2.9 %convolution_convert_fusion.1 = bf16[1024,896]{1,0:T(8,128)(2,1)S(1)} fusion(bf16[1024,512]{1,0:T(8,128)(2,1)S(1)} %bitcast.93, bf16[512,1792]{1,0:T(8,128)(2,1)} %param.13), kind=kOutput, calls=%fused_computation.23 | convolution fusion | flops 940441600 | bytes 3801088 | tf_op jit(solution)/shard_map/dot_general | solution.py:93
  33.8 0.8 dynamic-slice_bitcast_fusion
  34.6 1.9 collective-permute-start
  36.5 3.9 %collective-permute-start.1 = (bf16[128,896]{1,0:T(8,128)(2,1)}, bf16[128,896]{1,0:T(8,128)(2,1)S(1)}, u32[]{:S(2)}, u32[]{:S(2)}) collective-permute-start(bf16[128,896]{1,0:T(8,128)(2,1)} %get-tuple-element.48), channel_id=1, source_target_pairs={{0,56},{8,0},{16,8},{24,16},{32,24},{40,32},{48,40},{56,48},{1,57}... | collective-permute-start | bytes 688136 | tf_op jit(solution)/shard_map/ppermute | solution.py:12
  40.4 2.6 convolution_convert_fusion
  43.0 8.5 %collective-permute-done = bf16[128,896]{1,0:T(8,128)(2,1)S(1)} collective-permute-done((bf16[128,896]{1,0:T(8,128)(2,1)}, bf16[128,896]{1,0:T(8,128)(2,1)S(1)}, u32[]{:S(2)}, u32[]{:S(2)}) %collective-permute-start) | collective-permute-done | bytes 229408 | tf_op jit(solution)/shard_map/ppermute | solution.py:12
  51.6 0.9 fusion.43
  52.4 3.2 %collective-permute-start.3 = (bf16[128,896]{1,0:T(8,128)(2,1)}, bf16[128,896]{1,0:T(8,128)(2,1)S(1)}, u32[]{:S(2)}, u32[]{:S(2)}) collective-permute-start(bf16[128,896]{1,0:T(8,128)(2,1)} %get-tuple-element.46), channel_id=1, source_target_pairs={{0,56},{8,0},{16,8},{24,16},{32,24},{40,32},{48,40},{56,48},{1,57}... | collective-permute-start | bytes 688136 | tf_op jit(solution)/shard_map/ppermute | solution.py:12
  55.7 10.8 %collective-permute-done.2 = bf16[128,896]{1,0:T(8,128)(2,1)S(1)} collective-permute-done((bf16[128,896]{1,0:T(8,128)(2,1)}, bf16[128,896]{1,0:T(8,128)(2,1)S(1)}, u32[]{:S(2)}, u32[]{:S(2)}) %collective-permute-start.2) | collective-permute-done | bytes 229408 | tf_op jit(solution)/shard_map/ppermute | solution.py:12
  66.5 6.5 %all-gather.3.cloned.1.call-done = bf16[1024,1792]{1,0:T(8,128)(2,1)} async-done(((bf16[128,1792]{1,0:T(8,128)(2,1)}), bf16[1024,1792]{1,0:T(8,128)(2,1)}) %all-gather.3.cloned.1.call-update) | async-done | bytes 3670032 | tf_op jit(solution)/shard_map/all_gather | solution.py:90
  73.2 8.6 %collective-permute-done.4 = bf16[128,896]{1,0:T(8,128)(2,1)} collective-permute-done((bf16[128,896]{1,0:T(8,128)(2,1)S(1)}, bf16[128,896]{1,0:T(8,128)(2,1)}, u32[]{:S(2)}, u32[]{:S(2)}) %collective-permute-start.4) | collective-permute-done | bytes 229408 | tf_op jit(solution)/shard_map/ppermute | solution.py:12
  81.8 1.0 fusion.46
  83.1 1.9 collective-permute-start.5
  85.0 8.3 %collective-permute-done.6 = bf16[128,896]{1,0:T(8,128)(2,1)S(1)} collective-permute-done((bf16[128,896]{1,0:T(8,128)(2,1)S(1)}, bf16[128,896]{1,0:T(8,128)(2,1)S(1)}, u32[]{:S(2)}, u32[]{:S(2)}) %collective-permute-start.6) | collective-permute-done | bytes 229408 | tf_op jit(solution)/shard_map/ppermute | solution.py:12
  93.8 1.0 fusion.47
  95.1 0.8 constant_dynamic-update-slice_fusion.7
  96.0 2.0 collective-permute-start.8
  98.0 4.3 %fusion.56 = f32[1792,512]{0,1:T(8,128)S(1)} fusion(bf16[1024,1792]{1,0:T(8,128)(2,1)} %all-gather.3.cloned.1.call-done, bf16[1024,512]{1,0:T(8,128)(2,1)S(1)} %bitcast.95), kind=kOutput, calls=%fused_computation.99 | convolution fusion | flops 1879048192 | bytes 8388608 | tf_op jit(solution)/shard_map/dot_general | solution.py:61
  102.3 1.9 copy-done.5
  104.2 1.0 fusion.18
  105.2 14.9 %reduce-scatter.2.cloned.1.call-done = bf16[128,896]{1,0:T(8,128)(2,1)} async-done(((bf16[1024,896]{1,0:T(8,128)(2,1)}), bf16[128,896]{1,0:T(8,128)(2,1)}) %reduce-scatter.2.cloned.1.call-update) | async-done | bytes 229392 | tf_op jit(solution)/shard_map/reduce_scatter | solution.py:99
  120.2 1.2 fusion.26
  121.3 0.9 pad_maximum_fusion.1
  122.2 1.1 broadcast_in_dim.7
  123.4 5.7 %all-to-all-start.1 = ((bf16[8,128,512]{2,1,0:T(8,128)(2,1)}), bf16[8,128,512]{2,1,0:T(8,128)(2,1)S(1)}, u32[]{:S(2)}, u32[]{:S(2)}) async-start(bf16[8,128,512]{2,1,0:T(8,128)(2,1)} %broadcast_in_dim.7), calls=%async_computation.2 | async-start | bytes 2097152 | tf_op jit(solution)/shard_map/all_to_all | solution.py:16
  129.1 1.7 collective-permute-start.9
  131.1 1.9 bitcast_add_fusion.2
  133.2 2.8 collective-permute-start.12
  135.9 13.7 %collective-permute-done.9 = bf16[128,1792]{1,0:T(8,128)(2,1)S(1)} collective-permute-done((bf16[128,1792]{1,0:T(8,128)(2,1)S(1)}, bf16[128,1792]{1,0:T(8,128)(2,1)S(1)}, u32[]{:S(2)}, u32[]{:S(2)}) %collective-permute-start.9) | collective-permute-done | bytes 458784 | tf_op jit(solution)/shard_map/ppermute | solution.py:12
  149.6 3.7 %collective-permute-start.10 = (bf16[128,1792]{1,0:T(8,128)(2,1)S(1)}, bf16[128,1792]{1,0:T(8,128)(2,1)S(1)}, u32[]{:S(2)}, u32[]{:S(2)}) collective-permute-start(bf16[128,1792]{1,0:T(8,128)(2,1)S(1)} %collective-permute-done.9), channel_id=1, source_target_pairs={{0,56},{8,0},{16,8},{24,16},{32,24},{40,32},{48,40},{56,48},{1,57}... | collective-permute-start | bytes 1376264 | tf_op jit(solution)/shard_map/ppermute | solution.py:12
  153.3 0.8 constant_dynamic-update-slice_fusion.6
  154.1 0.8 constant_dynamic-update-slice_fusion.5
  155.0 17.7 %collective-permute-done.10 = bf16[128,1792]{1,0:T(8,128)(2,1)S(1)} collective-permute-done((bf16[128,1792]{1,0:T(8,128)(2,1)S(1)}, bf16[128,1792]{1,0:T(8,128)(2,1)S(1)}, u32[]{:S(2)}, u32[]{:S(2)}) %collective-permute-start.10) | collective-permute-done | bytes 458784 | tf_op jit(solution)/shard_map/ppermute | solution.py:12
  172.7 3.7 %collective-permute-start.13 = (bf16[128,1792]{1,0:T(8,128)(2,1)S(1)}, bf16[128,1792]{1,0:T(8,128)(2,1)S(1)}, u32[]{:S(2)}, u32[]{:S(2)}) collective-permute-start(bf16[128,1792]{1,0:T(8,128)(2,1)S(1)} %collective-permute-done.10), channel_id=1, source_target_pairs={{0,56},{8,0},{16,8},{24,16},{32,24},{40,32},{48,40},{56,48},{1,57}... | collective-permute-start | bytes 1376264 | tf_op jit(solution)/shard_map/ppermute | solution.py:12
  176.4 1.0 bitcast_add_fusion.3
  177.4 0.8 constant_dynamic-update-slice_fusion.4
  178.2 13.4 %collective-permute-done.13 = bf16[128,1792]{1,0:T(8,128)(2,1)S(1)} collective-permute-done((bf16[128,1792]{1,0:T(8,128)(2,1)S(1)}, bf16[128,1792]{1,0:T(8,128)(2,1)S(1)}, u32[]{:S(2)}, u32[]{:S(2)}) %collective-permute-start.13) | collective-permute-done | bytes 458784 | tf_op jit(solution)/shard_map/ppermute | solution.py:12
  191.6 0.8 constant_dynamic-update-slice_fusion.3
  192.4 0.8 constant_dynamic-update-slice_fusion.2
  194.8 4.7 %fusion.12 = f32[1792,512]{1,0:T(8,128)S(1)} fusion(bf16[1024,1792]{1,0:T(8,128)(2,1)} %constant_dynamic-update-slice_fusion, s32[]{:T(128)S(6)} %select_n.70, bf16[1024,512]{1,0:T(8,128)(2,1)S(1)} %bitcast.96), kind=kOutput, calls=%fused_computation.29 | convolution fusion | flops 1881145344 | bytes 8388612 | tf_op jit(solution)/shard_map/dot_general | solution.py:61
  199.6 1.9 copy-done
  201.5 1.0 fusion.19
  202.5 2.7 collective-permute-done.16
  205.2 1.8 fusion.9
  207.0 1.5 collective-permute-start.17
  208.6 1.5 fusion.54
  210.1 4.1 %fusion.1 = f32[1024,512]{1,0:T(8,128)S(1)} fusion(bf16[1024,1792]{1,0:T(8,128)(2,1)} %constant_dynamic-update-slice_fusion, bf16[896,512]{1,0:T(8,128)(2,1)S(1)} %get-tuple-element.56, bf16[896,512]{1,0:T(8,128)(2,1)S(1)} %get-tuple-element.41), kind=kOutput, calls=%fused_computation.6 | convolution fusion | flops 1882718208 | bytes 7602176 | tf_op jit(solution)/shard_map/dot_general | solution.py:122
  214.2 2.4 fusion
  216.6 16.2 %collective-permute-done.17 = bf16[2,448,512]{2,1,0:T(8,128)(2,1)S(1)} collective-permute-done((bf16[2,448,512]{2,1,0:T(8,128)(2,1)S(1)}, bf16[2,448,512]{2,1,0:T(8,128)(2,1)S(1)}, u32[]{:S(2)}, u32[]{:S(2)}) %collective-permute-start.17) | collective-permute-done | bytes 917536 | tf_op jit(solution)/shard_map/ppermute | solution.py:121
  233.2 4.6 %fusion.57 = f32[1792,512]{1,0:T(8,128)S(1)} fusion(bf16[1024,1792]{1,0:T(8,128)(2,1)} %all-gather.5.cloned.1.call-done, bf16[1024,512]{1,0:T(8,128)(2,1)} %bitcast.97), kind=kOutput, calls=%fused_computation.100 | convolution fusion | flops 1879048192 | bytes 8388608 | tf_op jit(solution)/shard_map/dot_general | solution.py:61
  238.1 2.5 collective-permute-done.18
  240.6 1.3 fusion.10
  241.9 2.4 collective-permute-start.19
  244.2 3.1 %add_convert_fusion = bf16[1024,512]{1,0:T(8,128)(2,1)} fusion(f32[1024,512]{1,0:T(8,128)S(1)} %copy-done.4, bf16[1024,1792]{1,0:T(8,128)(2,1)S(1)} %copy-done.16, bf16[896,512]{1,0:T(8,128)(2,1)S(1)} %copy-done.14, bf16[896,512]{1,0:T(8,128)(2,1)S(1)} %copy-done.13), kind=kOutput, calls=%fused_computation.5 | convolution fusion | flops 1883766784 | bytes 8650752 | tf_op jit(solution)/shard_map/dot_general | solution.py:131
  247.3 5.7 %all-to-all-start.2 = ((bf16[8,128,512]{2,1,0:T(8,128)(2,1)}), bf16[8,128,512]{2,1,0:T(8,128)(2,1)S(1)}, u32[]{:S(2)}, u32[]{:S(2)}) async-start(bf16[8,128,512]{2,1,0:T(8,128)(2,1)} %bitcast.98), calls=%async_computation.3 | async-start | bytes 2097152 | tf_op jit(solution)/shard_map/all_to_all | solution.py:16
  253.0 11.3 %collective-permute-done.19 = bf16[2,448,512]{2,1,0:T(8,128)(2,1)} collective-permute-done((bf16[2,448,512]{2,1,0:T(8,128)(2,1)}, bf16[2,448,512]{2,1,0:T(8,128)(2,1)}, u32[]{:S(2)}, u32[]{:S(2)}) %collective-permute-start.19) | collective-permute-done | bytes 917536 | tf_op jit(solution)/shard_map/ppermute | solution.py:133
  264.3 2.6 add_select_fusion
  266.9 1.4 slice_bitcast_fusion
  268.3 8.4 %all-to-all-done.2 = bf16[8,128,512]{2,1,0:T(8,128)(2,1)S(1)} async-done(((bf16[8,128,512]{2,1,0:T(8,128)(2,1)}), bf16[8,128,512]{2,1,0:T(8,128)(2,1)S(1)}, u32[]{:S(2)}, u32[]{:S(2)}) %all-to-all-start.2) | async-done | bytes 1048608 | tf_op jit(solution)/shard_map/all_to_all | solution.py:16
  276.7 0.8 reduce_sum.12
  (67 shorter events, 4.1 us)
Async XLA Ops:
  7.2 65.8 %all-gather.3.cloned.1.call-start = ((), (), s32[]{:S(2)}) async-start(), calls=%async_computation.5 | async-start | bytes 4128768 | tf_op jit(solution)/shard_map/all_gather | solution.py:90
  11.4 19.5 %all-to-all-start = ((bf16[8,128,512]{2,1,0:T(8,128)(2,1)}), bf16[8,128,512]{2,1,0:T(8,128)(2,1)S(1)}, u32[]{:S(2)}, u32[]{:S(2)}) async-start(bf16[8,128,512]{2,1,0:T(8,128)(2,1)} %broadcast_in_dim.6), calls=%async_computation | async-start | bytes 2097152 | tf_op jit(solution)/shard_map/all_to_all | solution.py:16
  17.3 102.9 %reduce-scatter.2.cloned.1.call-start = ((), (), s32[]{:S(2)}) async-start(), calls=%async_computation.4 | async-start | bytes 2064384 | tf_op jit(solution)/shard_map/reduce_scatter | solution.py:99
  30.9 9.5 %copy-start.10 = (bf16[8,128,512]{2,1,0:T(8,128)(2,1)}, bf16[8,128,512]{2,1,0:T(8,128)(2,1)S(1)}, u32[]{:S(2)}) copy-start(bf16[8,128,512]{2,1,0:T(8,128)(2,1)S(1)} %all-to-all-done) | copy-start | bytes 3145732
  30.9 9.5 %copy-start.17 = (bf16[512,1792]{1,0:T(8,128)(2,1)S(1)}, bf16[512,1792]{1,0:T(8,128)(2,1)}, u32[]{:S(2)}) copy-start(bf16[512,1792]{1,0:T(8,128)(2,1)} %param.13) | copy-start | bytes 5505028
  34.6 16.9 %collective-permute-start = (bf16[128,896]{1,0:T(8,128)(2,1)}, bf16[128,896]{1,0:T(8,128)(2,1)S(1)}, u32[]{:S(2)}, u32[]{:S(2)}) collective-permute-start(bf16[128,896]{1,0:T(8,128)(2,1)} %get-tuple-element.49), channel_id=1, source_target_pairs={{0,8},{8,16},{16,24},{24,32},{32,40},{40,48},{48,56},{56,0},{1,9},... | collective-permute-start | bytes 688136 | tf_op jit(solution)/shard_map/ppermute | solution.py:12
  36.5 15.0 %collective-permute-start.1 = (bf16[128,896]{1,0:T(8,128)(2,1)}, bf16[128,896]{1,0:T(8,128)(2,1)S(1)}, u32[]{:S(2)}, u32[]{:S(2)}) collective-permute-start(bf16[128,896]{1,0:T(8,128)(2,1)} %get-tuple-element.48), channel_id=1, source_target_pairs={{0,56},{8,0},{16,8},{24,16},{32,24},{40,32},{48,40},{56,48},{1,57}... | collective-permute-start | bytes 688136 | tf_op jit(solution)/shard_map/ppermute | solution.py:12
  51.5 181.7 %all-gather.5.cloned.1.call-start = ((), (), s32[]{:S(2)}) async-start(), calls=%async_computation.6 | async-start | bytes 4128768 | tf_op jit(solution)/shard_map/all_gather | solution.py:106
  51.5 43.3 %copy-start.8 = (bf16[128,1792]{1,0:T(8,128)(2,1)S(1)}, bf16[128,1792]{1,0:T(8,128)(2,1)}, u32[]{:S(2)}) copy-start(bf16[128,1792]{1,0:T(8,128)(2,1)} %param.10) | copy-start | bytes 1376260
  51.6 43.3 %copy-start.9 = (bf16[128,1792]{1,0:T(8,128)(2,1)S(1)}, bf16[128,1792]{1,0:T(8,128)(2,1)}, u32[]{:S(2)}) copy-start(bf16[128,1792]{1,0:T(8,128)(2,1)} %param.9) | copy-start | bytes 1376260
  52.4 14.0 %collective-permute-start.2 = (bf16[128,896]{1,0:T(8,128)(2,1)}, bf16[128,896]{1,0:T(8,128)(2,1)S(1)}, u32[]{:S(2)}, u32[]{:S(2)}) collective-permute-start(bf16[128,896]{1,0:T(8,128)(2,1)} %get-tuple-element.47), channel_id=1, source_target_pairs={{0,8},{8,16},{16,24},{24,32},{32,40},{40,48},{48,56},{56,0},{1,9},... | collective-permute-start | bytes 688136 | tf_op jit(solution)/shard_map/ppermute | solution.py:12
  52.4 14.0 %collective-permute-start.3 = (bf16[128,896]{1,0:T(8,128)(2,1)}, bf16[128,896]{1,0:T(8,128)(2,1)S(1)}, u32[]{:S(2)}, u32[]{:S(2)}) collective-permute-start(bf16[128,896]{1,0:T(8,128)(2,1)} %get-tuple-element.46), channel_id=1, source_target_pairs={{0,56},{8,0},{16,8},{24,16},{32,24},{40,32},{48,40},{56,48},{1,57}... | collective-permute-start | bytes 688136 | tf_op jit(solution)/shard_map/ppermute | solution.py:12
  73.1 8.7 %collective-permute-start.4 = (bf16[128,896]{1,0:T(8,128)(2,1)S(1)}, bf16[128,896]{1,0:T(8,128)(2,1)}, u32[]{:S(2)}, u32[]{:S(2)}) collective-permute-start(bf16[128,896]{1,0:T(8,128)(2,1)S(1)} %fusion.45), channel_id=1, source_target_pairs={{0,8},{8,16},{16,24},{24,32},{32,40},{40,48},{48,56},{56,0},{1,9},... | collective-permute-start | bytes 688136 | tf_op jit(solution)/shard_map/ppermute | solution.py:12
  82.9 10.4 %collective-permute-start.6 = (bf16[128,896]{1,0:T(8,128)(2,1)S(1)}, bf16[128,896]{1,0:T(8,128)(2,1)S(1)}, u32[]{:S(2)}, u32[]{:S(2)}) collective-permute-start(bf16[128,896]{1,0:T(8,128)(2,1)S(1)} %get-tuple-element.45), channel_id=1, source_target_pairs={{0,56},{8,0},{16,8},{24,16},{32,24},{40,32},{48,40},{56,48},{1,57}... | collective-permute-start | bytes 688136 | tf_op jit(solution)/shard_map/ppermute | solution.py:12
  83.1 10.7 %collective-permute-start.5 = (bf16[128,896]{1,0:T(8,128)(2,1)S(1)}, bf16[128,896]{1,0:T(8,128)(2,1)}, u32[]{:S(2)}, u32[]{:S(2)}) collective-permute-start(bf16[128,896]{1,0:T(8,128)(2,1)S(1)} %get-tuple-element.44), channel_id=1, source_target_pairs={{0,8},{8,16},{16,24},{24,32},{32,40},{40,48},{48,56},{56,0},{1,9},... | collective-permute-start | bytes 688136 | tf_op jit(solution)/shard_map/ppermute | solution.py:12
  85.0 13.0 %copy-start.11 = (bf16[8,128,512]{2,1,0:T(8,128)(2,1)S(1)}, bf16[8,128,512]{2,1,0:T(8,128)(2,1)}, u32[]{:S(2)}) copy-start(bf16[8,128,512]{2,1,0:T(8,128)(2,1)} %copy-done.10) | copy-start | bytes 3145732
  96.0 24.2 %collective-permute-start.7 = (bf16[128,1792]{1,0:T(8,128)(2,1)S(1)}, bf16[128,1792]{1,0:T(8,128)(2,1)S(1)}, u32[]{:S(2)}, u32[]{:S(2)}) collective-permute-start(bf16[128,1792]{1,0:T(8,128)(2,1)S(1)} %get-tuple-element.55), channel_id=1, source_target_pairs={{0,56},{8,0},{16,8},{24,16},{32,24},{40,32},{48,40},{56,48},{1,57}... | collective-permute-start | bytes 1376264 | tf_op jit(solution)/shard_map/ppermute | solution.py:12
  96.0 24.2 %collective-permute-start.8 = (bf16[128,1792]{1,0:T(8,128)(2,1)S(1)}, bf16[128,1792]{1,0:T(8,128)(2,1)S(1)}, u32[]{:S(2)}, u32[]{:S(2)}) collective-permute-start(bf16[128,1792]{1,0:T(8,128)(2,1)S(1)} %get-tuple-element.55), channel_id=1, source_target_pairs={{0,8},{8,16},{16,24},{24,32},{32,40},{40,48},{48,56},{56,0},{1,9},... | collective-permute-start | bytes 1376264 | tf_op jit(solution)/shard_map/ppermute | solution.py:12
  102.3 1.9 copy-start.5
  104.2 18.0 %copy-start.15 = (bf16[128,512]{1,0:T(8,128)(2,1)S(1)}, bf16[128,512]{1,0:T(8,128)(2,1)}, u32[]{:S(2)}) copy-start(bf16[128,512]{1,0:T(8,128)(2,1)} %param.7) | copy-start | bytes 393220
  105.2 25.9 %collective-permute-start.11 = (bf16[2,128,1792]{2,1,0:T(8,128)(2,1)}, bf16[2,128,1792]{2,1,0:T(8,128)(2,1)}, u32[]{:S(2)}, u32[]{:S(2)}) collective-permute-start(bf16[2,128,1792]{2,1,0:T(8,128)(2,1)} %fusion.18), channel_id=1, source_target_pairs={{0,64},{64,0},{128,192},{192,128},{1,65},{65,1},{129,193},{193,129... | collective-permute-start | bytes 2752520 | tf_op jit(solution)/shard_map/ppermute | solution.py:28
  123.4 71.4 %all-to-all-start.1 = ((bf16[8,128,512]{2,1,0:T(8,128)(2,1)}), bf16[8,128,512]{2,1,0:T(8,128)(2,1)S(1)}, u32[]{:S(2)}, u32[]{:S(2)}) async-start(bf16[8,128,512]{2,1,0:T(8,128)(2,1)} %broadcast_in_dim.7), calls=%async_computation.2 | async-start | bytes 2097152 | tf_op jit(solution)/shard_map/all_to_all | solution.py:16
  129.1 20.5 %collective-permute-start.9 = (bf16[128,1792]{1,0:T(8,128)(2,1)S(1)}, bf16[128,1792]{1,0:T(8,128)(2,1)S(1)}, u32[]{:S(2)}, u32[]{:S(2)}) collective-permute-start(bf16[128,1792]{1,0:T(8,128)(2,1)S(1)} %collective-permute-done.7), channel_id=1, source_target_pairs={{0,56},{8,0},{16,8},{24,16},{32,24},{40,32},{48,40},{56,48},{1,57}... | collective-permute-start | bytes 1376264 | tf_op jit(solution)/shard_map/ppermute | solution.py:12
  130.8 23.4 %collective-permute-start.14 = (bf16[128,1792]{1,0:T(8,128)(2,1)S(1)}, bf16[128,1792]{1,0:T(8,128)(2,1)S(1)}, u32[]{:S(2)}, u32[]{:S(2)}) collective-permute-start(bf16[128,1792]{1,0:T(8,128)(2,1)S(1)} %collective-permute-done.8), channel_id=1, source_target_pairs={{0,8},{8,16},{16,24},{24,32},{32,40},{40,48},{48,56},{56,0},{1,9},... | collective-permute-start | bytes 1376264 | tf_op jit(solution)/shard_map/ppermute | solution.py:12
  133.2 43.2 %collective-permute-start.12 = (bf16[128,1792]{1,0:T(8,128)(2,1)S(1)}, bf16[128,1792]{1,0:T(8,128)(2,1)S(1)}, u32[]{:S(2)}, u32[]{:S(2)}) collective-permute-start(bf16[128,1792]{1,0:T(8,128)(2,1)S(1)} %fusion.41), channel_id=1, source_target_pairs={{0,128},{128,0},{64,192},{192,64},{1,129},{129,1},{65,193},{193,65... | collective-permute-start | bytes 1376264 | tf_op jit(solution)/shard_map/ppermute | solution.py:112
  149.6 23.1 %collective-permute-start.10 = (bf16[128,1792]{1,0:T(8,128)(2,1)S(1)}, bf16[128,1792]{1,0:T(8,128)(2,1)S(1)}, u32[]{:S(2)}, u32[]{:S(2)}) collective-permute-start(bf16[128,1792]{1,0:T(8,128)(2,1)S(1)} %collective-permute-done.9), channel_id=1, source_target_pairs={{0,56},{8,0},{16,8},{24,16},{32,24},{40,32},{48,40},{56,48},{1,57}... | collective-permute-start | bytes 1376264 | tf_op jit(solution)/shard_map/ppermute | solution.py:12
  154.1 38.3 %collective-permute-start.15 = (bf16[128,1792]{1,0:T(8,128)(2,1)S(1)}, bf16[128,1792]{1,0:T(8,128)(2,1)S(1)}, u32[]{:S(2)}, u32[]{:S(2)}) collective-permute-start(bf16[128,1792]{1,0:T(8,128)(2,1)S(1)} %collective-permute-done.14), channel_id=1, source_target_pairs={{0,8},{8,16},{16,24},{24,32},{32,40},{40,48},{48,56},{56,0},{1,9},... | collective-permute-start | bytes 1376264 | tf_op jit(solution)/shard_map/ppermute | solution.py:12
  172.7 18.9 %collective-permute-start.13 = (bf16[128,1792]{1,0:T(8,128)(2,1)S(1)}, bf16[128,1792]{1,0:T(8,128)(2,1)S(1)}, u32[]{:S(2)}, u32[]{:S(2)}) collective-permute-start(bf16[128,1792]{1,0:T(8,128)(2,1)S(1)} %collective-permute-done.10), channel_id=1, source_target_pairs={{0,56},{8,0},{16,8},{24,16},{32,24},{40,32},{48,40},{56,48},{1,57}... | collective-permute-start | bytes 1376264 | tf_op jit(solution)/shard_map/ppermute | solution.py:12
  194.8 4.8 %copy-start.12 = (bf16[8,128,512]{2,1,0:T(8,128)(2,1)}, bf16[8,128,512]{2,1,0:T(8,128)(2,1)S(1)}, u32[]{:S(2)}) copy-start(bf16[8,128,512]{2,1,0:T(8,128)(2,1)S(1)} %all-to-all-done.1) | copy-start | bytes 3145732
  199.6 1.9 copy-start
  202.5 6.0 %copy-start.6 = (bf16[1792,512]{1,0:T(8,128)(2,1)S(1)}, bf16[1792,512]{1,0:T(8,128)(2,1)}, u32[]{:S(2)}) copy-start(bf16[1792,512]{1,0:T(8,128)(2,1)} %param.11) | copy-start | bytes 5505028
  202.5 2.7 collective-permute-start.16
  202.5 6.0 %copy-start.7 = (bf16[1792,512]{1,0:T(8,128)(2,1)S(1)}, bf16[1792,512]{1,0:T(8,128)(2,1)}, u32[]{:S(2)}) copy-start(bf16[1792,512]{1,0:T(8,128)(2,1)} %param.12) | copy-start | bytes 5505028
  207.0 25.8 %collective-permute-start.17 = (bf16[2,448,512]{2,1,0:T(8,128)(2,1)S(1)}, bf16[2,448,512]{2,1,0:T(8,128)(2,1)S(1)}, u32[]{:S(2)}, u32[]{:S(2)}) collective-permute-start(bf16[2,448,512]{2,1,0:T(8,128)(2,1)S(1)} %fusion.9), channel_id=1, source_target_pairs={{128,0},{192,64},{129,1},{193,65},{130,2},{194,66},{131,3},{195,67... | collective-permute-start | bytes 2752520 | tf_op jit(solution)/shard_map/ppermute | solution.py:121
  214.2 18.6 %copy-start.1 = (f32[1792,512]{1,0:T(8,128)S(1)}, f32[1792,512]{1,0:T(8,128)}, u32[]{:S(2)}) copy-start(f32[1792,512]{1,0:T(8,128)} %copy-done) | copy-start | bytes 11010052
  233.2 11.0 %copy-start.16 = (bf16[1024,1792]{1,0:T(8,128)(2,1)S(1)}, bf16[1024,1792]{1,0:T(8,128)(2,1)}, u32[]{:S(2)}) copy-start(bf16[1024,1792]{1,0:T(8,128)(2,1)} %all-gather.5.cloned.1.call-done) | copy-start | bytes 11010052
  237.8 4.0 %copy-start.2 = (f32[1792,512]{1,0:T(8,128)}, f32[1792,512]{1,0:T(8,128)S(1)}, u32[]{:S(2)}) copy-start(f32[1792,512]{1,0:T(8,128)S(1)} %fusion.57) | copy-start | bytes 11010052
  237.9 6.4 %copy-start.14 = (bf16[896,512]{1,0:T(8,128)(2,1)S(1)}, bf16[896,512]{1,0:T(8,128)(2,1)}, u32[]{:S(2)}) copy-start(bf16[896,512]{1,0:T(8,128)(2,1)} %get-tuple-element.57) | copy-start | bytes 2752516
  238.0 6.2 %copy-start.4 = (f32[1024,512]{1,0:T(8,128)S(1)}, f32[1024,512]{1,0:T(8,128)}, u32[]{:S(2)}) copy-start(f32[1024,512]{1,0:T(8,128)} %fusion) | copy-start | bytes 6291460
  238.0 6.2 %copy-start.13 = (bf16[896,512]{1,0:T(8,128)(2,1)S(1)}, bf16[896,512]{1,0:T(8,128)(2,1)}, u32[]{:S(2)}) copy-start(bf16[896,512]{1,0:T(8,128)(2,1)} %get-tuple-element.40) | copy-start | bytes 2752516
  238.0 2.6 collective-permute-start.18
  240.6 3.6 %copy-start.3 = (bf16[2,448,512]{2,1,0:T(8,128)(2,1)}, bf16[2,448,512]{2,1,0:T(8,128)(2,1)S(1)}, u32[]{:S(2)}) copy-start(bf16[2,448,512]{2,1,0:T(8,128)(2,1)S(1)} %collective-permute-done.18) | copy-start | bytes 2752516
  241.9 22.4 %collective-permute-start.19 = (bf16[2,448,512]{2,1,0:T(8,128)(2,1)}, bf16[2,448,512]{2,1,0:T(8,128)(2,1)}, u32[]{:S(2)}, u32[]{:S(2)}) collective-permute-start(bf16[2,448,512]{2,1,0:T(8,128)(2,1)} %fusion.10), channel_id=1, source_target_pairs={{0,128},{64,192},{1,129},{65,193},{2,130},{66,194},{3,131},{67,195... | collective-permute-start | bytes 2752520 | tf_op jit(solution)/shard_map/ppermute | solution.py:133
  247.3 29.4 %all-to-all-start.2 = ((bf16[8,128,512]{2,1,0:T(8,128)(2,1)}), bf16[8,128,512]{2,1,0:T(8,128)(2,1)S(1)}, u32[]{:S(2)}, u32[]{:S(2)}) async-start(bf16[8,128,512]{2,1,0:T(8,128)(2,1)} %bitcast.98), calls=%async_computation.3 | async-start | bytes 2097152 | tf_op jit(solution)/shard_map/all_to_all | solution.py:16
Sparse Core Ops, SparseCore 0:
  10.4 62.6 all-gather.2
  75.6 44.5 reduce-scatter.1
  122.3 70.9 all-gather.4
